TPU v7x, 32 devices: a whole 2x2x4 slice. The times are simulated.
32 devices in a mesh: dp: 4 (over y, x), mp: 8 (over z, core).
Axes of the slice: x: 2, y: 2, z: 4, core: 2. Of those that a mesh axis runs over, the one named last changes fastest.
Arguments:
- attn_input: bfloat16 [1024, 5120], P('dp'), may hold values from -8 to 8
- attn_gain: float32 [5120], replicated, may hold values from 0.1 to 1.9
- qkv_weight: float32 [5120, 6144], P(('dp', 'mp')), may hold values from -0.2 to 0.2
- mlp_input: bfloat16 [1024, 5120], P('dp'), may hold values from -6 to 6
- mlp_gain: float32 [5120], replicated, may hold values from 0.1 to 1.9
- gate_up_weight: float32 [5120, 32768], P(('dp', 'mp')), may hold values from -0.078125 to 0.078125
- prompt_lengths: int32 [6], replicated, may hold values from 1 to 512, 1024 in all
- request_prompt: int32 [64], replicated, may hold values from 0 to 5, as said below
- page_table: int32 [64, 4], replicated, may hold values from 0 to 383, as said below
Outputs:
- attended: bfloat16 [1024, 4096], P('dp', 'mp')
- hidden: bfloat16 [1024, 16384], P('dp', 'mp')
- kv_cache: bfloat16 [384, 128, 2048], P('dp', None, 'mp')
Inputs may be any that keep to these rules, and one draw needn't show every extreme that they name: `prompt_lengths`: the lengths sum to 1024. `request_prompt`: each of the 6 prompts is named by 8 to 16 requests. `page_table`: all entries are distinct.
All inputs are finite; a program needn't handle non-finite values.
Results may differ from a plain program's by a relative error of at most 0.009.
Values may be sent and summed in bfloat16 or wider, within the bound.
No kernel may reach another device: no remote copies, remote signals or barrier semaphores. Data moves between devices by JAX's collectives and lax.ppermute only.
A program may use at most 192 MiB of HBM per device.

v0:
```python
import functools

import jax
import jax.numpy as jnp
from jax import lax
from jax.experimental import pallas as pl
from jax.experimental.pallas import tpu as pltpu
from jax.sharding import PartitionSpec as P

HEADS = 32
KVH = 8
HD = 128
PAGE = 128
EPS = 1e-05
THETA = 100000000.0
SLOT_DEV = 96
SLOT_GROUP = 8
TOKEN_ROWS = 64
SMALL = pl.CostEstimate(flops=1, transcendentals=0, bytes_accessed=1)


def rms_norm(stream, gain_row):
    widened = stream.astype(jnp.float32)
    squares = jnp.mean(widened * widened, axis=-1, keepdims=True)
    return (widened * lax.rsqrt(squares + EPS) * gain_row).astype(jnp.bfloat16)


def swap(value, axis, offset):
    ways = lax.axis_size(axis)
    return lax.ppermute(value, axis, [(i, i ^ offset) for i in range(ways)])


def bits_of(ways):
    return [1 << i for i in range(ways.bit_length() - 1)]


def member_order(group):
    return [*range(0, group, 2), *range(1, group, 2)]


def token_cells(streams, gains, rows):
    data_ways = lax.axis_size("dp")
    group = lax.axis_size("mp") // 2
    data_at, model_at = lax.axis_index("dp"), lax.axis_index("mp")
    cells = []
    for stream, gain_row in zip(streams, gains):
        tokens = stream.shape[0]
        half = lax.dynamic_index_in_dim(
            rms_norm(stream, gain_row).reshape(tokens, data_ways, 2, group, rows),
            model_at // group,
            2,
            keepdims=False,
        )
        members = jnp.array(member_order(group), dtype=jnp.int32) ^ (model_at % group)
        half = jnp.take(half, members, axis=2).transpose(1, 0, 2, 3)
        cells.append(half.reshape(data_ways, tokens, group * rows))
    own = [lax.dynamic_index_in_dim(cell, data_at, 0, keepdims=False) for cell in cells]
    both = jnp.stack(cells, axis=1)
    away = [
        lax.dynamic_index_in_dim(both, data_at ^ s, 0, keepdims=False) for s in range(1, data_ways)
    ]
    return [*own, *away]


def token_kernel(at_ref, *refs, group, rows, streams):
    data_at, side, member = at_ref[0], at_ref[1], at_ref[2]
    width = group * rows
    own_refs = refs[2 * streams : 3 * streams]
    away_refs = refs[3 * streams :]
    for k in range(streams):
        stream_ref, gain_ref = refs[k], refs[streams + k]
        widened = stream_ref[...].astype(jnp.float32)
        scale = lax.rsqrt(jnp.mean(widened * widened, axis=-1, keepdims=True) + EPS)
        for s in range(len(away_refs) + 1):
            start = pl.multiple_of(((data_at ^ s) * 2 + side) * width, 128)
            block = stream_ref[:, pl.ds(start, width)].astype(jnp.float32)
            block = (block * scale * gain_ref[:, pl.ds(start, width)]).astype(jnp.bfloat16)
            pieces = [block[:, i * rows : (i + 1) * rows] for i in range(group)]
            for bit in bits_of(group):
                pieces = [
                    jnp.where((member & bit) != 0, pieces[i ^ bit], pieces[i]) for i in range(group)
                ]
            block = jnp.concatenate([pieces[i] for i in member_order(group)], axis=1)
            if s == 0:
                own_refs[k][...] = block
            else:
                away_refs[s - 1][k] = block


def token_cells_kernel(streams, gains, rows):
    data_ways = lax.axis_size("dp")
    group = lax.axis_size("mp") // 2
    tokens, depth = streams[0].shape
    count = len(streams)
    step = TOKEN_ROWS
    model_at = lax.axis_index("mp")
    at = jnp.stack([lax.axis_index("dp"), model_at // group, model_at % group]).astype(jnp.int32)
    width = group * rows
    return pl.pallas_call(
        functools.partial(token_kernel, group=group, rows=rows, streams=count),
        grid_spec=pltpu.PrefetchScalarGridSpec(
            num_scalar_prefetch=1,
            grid=(tokens // step,),
            in_specs=[pl.BlockSpec((step, depth), lambda i, at: (i, 0))] * count
            + [pl.BlockSpec((1, depth), lambda i, at: (0, 0))] * count,
            out_specs=[pl.BlockSpec((step, width), lambda i, at: (i, 0))] * count
            + [pl.BlockSpec((count, step, width), lambda i, at: (0, i, 0))] * (data_ways - 1),
        ),
        out_shape=[jax.ShapeDtypeStruct((tokens, width), jnp.bfloat16)] * count
        + [jax.ShapeDtypeStruct((count, tokens, width), jnp.bfloat16)] * (data_ways - 1),
        cost_estimate=SMALL,
        name="token_cells",
    )(at, *streams, *[gain_row[None] for gain_row in gains])


class Tokens:
    def __init__(self, order, streams, gains, rows):
        aligned = (lax.axis_size("mp") // 2 * rows) % 128 == 0
        streams = order.tie(*streams)
        cells = (token_cells_kernel if aligned else token_cells)(streams, gains, rows)
        self.order, self.own = order, cells[: len(streams)]
        order.done(self.own[0])
        self.away = [swap(cell, "dp", s + 1) for s, cell in enumerate(cells[len(streams) :])]

    def blocks(self):
        away = self.order.tie(*self.away)
        return [[own, *[block[k] for block in away]] for k, own in enumerate(self.own)]


def copy_kernel(at_ref, *refs, members):
    for s in range(members):
        refs[members + s % 2][s // 2] = refs[s][...].astype(jnp.bfloat16)


def pack_columns(weight, starts, width):
    group = lax.axis_size("mp") // 2
    rows = weight.shape[0]
    count = len(starts)

    def spec(s):
        def place(i, at):
            device = ((at[0] // group) ^ (i % (2 * parts) // parts)) * group + ((at[0] % group) ^ s)
            column = starts[0](device)
            which = i // (2 * parts) * parts + i % parts
            for k in range(1, count):
                column = jnp.where(which == k, starts[k](device), column)
            return 0, pl.multiple_of(column, 128)

        return pl.BlockSpec((pl.Element(rows), pl.Element(width)), place)

    parts = 2 if count % 2 == 0 else 1
    steps = 2 * count
    out = jax.ShapeDtypeStruct((group // 2, rows, steps * width), jnp.bfloat16)
    return pl.pallas_call(
        functools.partial(copy_kernel, members=group),
        grid_spec=pltpu.PrefetchScalarGridSpec(
            num_scalar_prefetch=1,
            grid=(steps,),
            in_specs=[spec(s) for s in range(group)],
            out_specs=[pl.BlockSpec((group // 2, rows, width), lambda i, at: (0, 0, i))] * 2,
        ),
        out_shape=[out] * 2,
        cost_estimate=SMALL,
        name="pack_columns",
    )(lax.axis_index("mp")[None].astype(jnp.int32), *[weight] * group)


def heads_copy_kernel(at_ref, *refs, members, parts):
    for s in range(members):
        done = 0
        for p in range(parts):
            block = refs[s * parts + p][...].astype(jnp.bfloat16)
            refs[members * parts + s % 2][s // 2, :, done : done + block.shape[1]] = block
            done += block.shape[1]


def pack_heads(weight, head_starts):
    group = lax.axis_size("mp") // 2
    rows = weight.shape[0]
    heads = len(head_starts(0))
    widths = [(heads - 2) * HD, HD, HD]

    def spec(s, part):
        def place(i, at):
            device = ((at[0] // group) ^ i) * group + ((at[0] % group) ^ s)
            found = head_starts(device)
            return 0, (found[0] // (heads - 2) if part == 0 else found[part - 3])

        return pl.BlockSpec((rows, widths[part]), place)

    out = jax.ShapeDtypeStruct((group // 2, rows, 2 * heads * HD), jnp.bfloat16)
    return pl.pallas_call(
        functools.partial(heads_copy_kernel, members=group, parts=3),
        grid_spec=pltpu.PrefetchScalarGridSpec(
            num_scalar_prefetch=1,
            grid=(2,),
            in_specs=[spec(s, part) for s in range(group) for part in range(3)],
            out_specs=[pl.BlockSpec((group // 2, rows, heads * HD), lambda i, at: (0, 0, i))] * 2,
        ),
        out_shape=[out] * 2,
        cost_estimate=SMALL,
        name="pack_heads",
    )(lax.axis_index("mp")[None].astype(jnp.int32), *[weight] * (3 * group))


class Order:
    def __init__(self):
        self.last = []

    def done(self, *values):
        self.last = list(values)

    def tie(self, *values):
        return lax.optimization_barrier((*values, *self.last))[: len(values)]


class Job:
    def __init__(self, order, width, finish):
        self.order, self.width, self.finish = order, width, finish
        self.bits = bits_of(lax.axis_size("dp"))
        self.waiting = [None, None]
        self.columns = slice(None)
        self.stored = None

    def send_weights(self):
        near, far = (array[:, :, self.columns] for array in self.order.tie(*self.stored))
        self.near, self.far_core = [near[0]], [far[0]]
        self.packets = []
        for s in range(1, near.shape[0]):
            payload = jnp.stack([near[s], far[s]])
            self.order.done(payload)
            self.packets.append(swap(payload, "mp", 2 * s))

    def join_weights(self, others=()):
        stored = [array for job in others for array in job.stored]
        ready = self.order.tie(*self.packets, *stored)
        packets, stored = ready[: len(self.packets)], ready[len(self.packets) :]
        for i, job in enumerate(others):
            job.stored = stored[2 * i : 2 * i + 2]
        rows = [*self.near, *[p[0] for p in packets], *self.far_core, *[p[1] for p in packets]]
        self.weights = [
            jnp.concatenate([part[:, a * self.width : (a + 1) * self.width] for part in rows])
            for a in range(2)
        ]
        every = range(lax.axis_size("dp"))
        self.arrived = [{s: [] for s in every} for _ in range(2)]
        self.remaining = [list(every) for _ in range(2)]
        self.order.done(self.weights[0])

    def partial(self, half, which):
        blocks = self.blocks
        left = blocks[which[0]] if len(which) == 1 else jnp.concatenate([blocks[s] for s in which])
        return jnp.dot(left, self.weights[half], preferred_element_type=jnp.float32)

    def total(self, half, which, partial):
        for parts in zip(*[self.arrived[half][s] for s in which]):
            joined = parts[0] if len(which) == 1 else jnp.concatenate(parts)
            partial = partial + joined.astype(jnp.float32)
        return partial

    def product(self, half, which):
        return self.total(half, which, self.partial(half, which))

    def prepare(self, half, level):
        bit = (self.bits[::-1] if half else self.bits)[level]
        leaving = [s for s in self.remaining[half] if s & bit]
        self.remaining[half] = [s for s in self.remaining[half] if not s & bit]
        partial = self.partial(half, leaving)
        return leaving, bit, partial.astype(jnp.bfloat16) if level == 0 else partial

    def leave(self, half, prepared):
        leaving, bit, partial = prepared
        self.waiting[half] = [s ^ bit for s in leaving]
        return self.total(half, leaving, partial).astype(jnp.bfloat16)

    def land(self, half, received):
        tokens = received.shape[0] // len(self.waiting[half])
        for i, s in enumerate(self.waiting[half]):
            self.arrived[half][s].append(received[i * tokens : (i + 1) * tokens])

    def last_far(self):
        (partial,) = self.order.tie(self.partial(1, [0]))
        far = self.total(1, [0], partial).astype(jnp.bfloat16)
        self.order.done(far)
        self.far = swap(far, "mp", lax.axis_size("mp") // 2)

    def close(self):
        far, partial = self.order.tie(self.far, self.partial(0, [0]))
        self.result = self.finish(self.total(0, [0], partial), far)
        self.order.done(self.result)


def feed_forward_jobs(order, cols, side_width):
    width = min(side_width // 2, cols) // 128 * 128
    widths = [width] * (cols // width) + ([cols % width] if cols % width else [])

    def finish_for(width):
        def finish(near, far):
            both = near + far.astype(jnp.float32)
            return (jax.nn.silu(both[:, :width]) * both[:, width:]).astype(jnp.bfloat16)

        return finish

    jobs = []
    for at, width in enumerate(widths):
        jobs.append(Job(order, 2 * width, finish_for(width)))
        jobs[-1].offset = sum(widths[:at])
    return jobs


def store_feed_forward(order, members, weight, cols):
    half_cols = weight.shape[1] // 2
    width = members[0].width // 2
    starts = []
    for job in members:
        for base in (0, half_cols):
            starts.append(lambda device, at=base + job.offset: device * cols + at)
    (weight,) = order.tie(weight)
    near, far = pack_columns(weight, starts, width)
    order.done(near)
    far = swap(far, "mp", 1)
    for k, job in enumerate(members):
        job.stored, job.columns = (near, far), slice(k * 4 * width, (k + 1) * 4 * width)


def run_jobs(jobs, last_jobs, store_last, early, late):
    order, bits = jobs[0].order, jobs[0].bits
    levels, count = len(bits), len(jobs)
    flying = []
    for turn in range(count + levels + 1):
        if 0 < turn < count:
            jobs[turn].join_weights(last_jobs[:1] if turn == 1 else ())
            for job in last_jobs[1:] if turn == 1 else ():
                job.stored = last_jobs[0].stored
        for extra in early.get(turn, ()):
            extra()
        riders = []
        for level in range(levels):
            for half in (1, 0):
                if 0 <= turn - level < count:
                    job = jobs[turn - level]
                    riders.append((half, job, job.prepare(half, level)))
        ready = order.tie(
            *[received for received, _ in flying], *[prepared[2] for _, _, prepared in riders]
        )
        landed, partials = ready[: len(flying)], ready[len(flying) :]
        riders = [
            (half, job, (*prepared[:2], partial))
            for (half, job, prepared), partial in zip(riders, partials)
        ]
        for received, (_, members) in zip(landed, flying):
            at = 0
            for half, job, size in members:
                job.land(half, received[at : at + size])
                at += size
        flying = []
        grouped = {}
        for half, job, prepared in riders:
            part = job.leave(half, prepared)
            grouped.setdefault((prepared[1], job.width), []).append((half, job, part))
        payloads = [
            parts[0][2] if len(parts) == 1 else jnp.concatenate([part for _, _, part in parts])
            for parts in grouped.values()
        ]
        if payloads:
            order.done(*payloads)
        for ((bit, _), parts), payload in zip(grouped.items(), payloads):
            members = [(half, job, part.shape[0]) for half, job, part in parts]
            flying.append((swap(payload, "dp", bit), members))
        if turn + 2 < count and turn > levels:
            jobs[turn - levels - 1].close()
        if 0 <= turn - levels < count:
            jobs[turn - levels].last_far()
        if turn + 2 < count:
            jobs[turn + 2].send_weights()
        elif turn > levels:
            jobs[turn - levels - 1].close()
        if turn == 0:
            store_last()
        for extra in late.get(turn, ()):
            extra()


def heads_kernel(near_ref, far_ref, cos_ref, sin_ref, q_ref, kv_ref):
    turned = (near_ref.shape[1] // HD) - 1
    for h in range(turned + 1):
        at = slice(h * HD, (h + 1) * HD)
        head = near_ref[:, at] + far_ref[:, at].astype(jnp.float32)
        if h < turned:
            head = head * cos_ref[...] + pltpu.roll(head, HD // 2, 1) * sin_ref[...]
        if h < turned - 1:
            q_ref[:, at] = head.astype(jnp.bfloat16)
        else:
            kv_ref[:, (h + 1 - turned) * HD : (h + 2 - turned) * HD] = head.astype(jnp.bfloat16)


def finish_heads(near, far, positions):
    half_dim = HD // 2
    frequency = THETA ** (-jnp.arange(half_dim, dtype=jnp.float32) / half_dim)
    angles = positions.astype(jnp.float32)[:, None] * frequency[None, :]
    cosine, sine = jnp.cos(angles), jnp.sin(angles)
    tokens, width = near.shape
    return pl.pallas_call(
        heads_kernel,
        out_shape=[
            jax.ShapeDtypeStruct((tokens, width - 2 * HD), jnp.bfloat16),
            jax.ShapeDtypeStruct((tokens, 2 * HD), jnp.bfloat16),
        ],
        cost_estimate=SMALL,
        name="finish_heads",
    )(
        near,
        far,
        jnp.concatenate([cosine, cosine], axis=1),
        jnp.concatenate([-sine, sine], axis=1),
    )


def gather_rows(at_ref, piece_refs, rows_ref):
    tokens = piece_refs[0].shape[0]
    s = 0
    for piece_ref in piece_refs:
        for i in range(piece_ref.shape[0] // tokens):
            start = pl.multiple_of((at_ref[0] ^ s) * tokens, 128)
            block = piece_ref[i * tokens : (i + 1) * tokens, :]
            rows_ref[pl.ds(start, tokens), :] = block.astype(rows_ref.dtype)
            s += 1


def attend_kernel(at_ref, q_ref, first_ref, token_ref, *refs):
    *piece_refs, out_ref, rows_ref = refs

    @pl.when(pl.program_id(0) == 0)
    def _():
        gather_rows(at_ref, piece_refs, rows_ref)

    scores = lax.dot_general(
        q_ref[...],
        rows_ref[:, :HD],
        (((1,), (1,)), ((), ())),
        preferred_element_type=jnp.float32,
    ) * HD ** (-0.5)
    key_ids = lax.broadcasted_iota(jnp.int32, scores.shape, 1)
    allowed = (key_ids >= first_ref[...]) & (key_ids <= token_ref[...])
    scores = jnp.where(allowed, scores, -jnp.inf)
    peak = jnp.max(scores, axis=-1, keepdims=True)
    weights = jnp.exp(scores - peak)
    probs = (weights / jnp.sum(weights, axis=-1, keepdims=True)).astype(jnp.bfloat16)
    attended = jnp.dot(probs, rows_ref[:, HD:], preferred_element_type=jnp.float32)
    out_ref[...] = attended.astype(jnp.bfloat16)


def attend(queries, pieces, first, token, at):
    tokens, width = queries.shape
    total = sum(piece.shape[0] for piece in pieces)
    heads = width // HD
    return pl.pallas_call(
        attend_kernel,
        grid_spec=pltpu.PrefetchScalarGridSpec(
            num_scalar_prefetch=1,
            grid=(heads,),
            in_specs=[
                pl.BlockSpec((tokens, HD), lambda h, at: (0, h)),
                pl.BlockSpec((tokens, 1), lambda h, at: (0, 0)),
                pl.BlockSpec((tokens, 1), lambda h, at: (0, 0)),
                *[pl.BlockSpec(piece.shape, lambda h, at: (0, 0)) for piece in pieces],
            ],
            out_specs=pl.BlockSpec((tokens, HD), lambda h, at: (0, h)),
            scratch_shapes=[pltpu.VMEM((total, 2 * HD), jnp.bfloat16)],
        ),
        out_shape=jax.ShapeDtypeStruct((tokens, width), jnp.bfloat16),
        cost_estimate=SMALL,
        name="attend",
    )(at, queries, first, token, *pieces)


def pages_kernel(at_ref, start_ref, count_ref, *refs):
    *piece_refs, out_ref, rows_ref = refs
    group = out_ref.shape[0]

    @pl.when(pl.program_id(0) == 0)
    def _():
        gather_rows(at_ref, piece_refs, rows_ref)
        tail = rows_ref.shape[0] - PAGE
        rows_ref[tail:, :] = jnp.zeros((PAGE, rows_ref.shape[1]), rows_ref.dtype)

    base = pl.program_id(0) * group

    def fill(i, carry):
        start = start_ref[base + i]
        shift = lax.rem(start, 8)
        tall = rows_ref[pl.ds(pl.multiple_of(start - shift, 8), PAGE + 8), :]
        page = pltpu.roll(tall, lax.rem(PAGE + 8 - shift, PAGE + 8), 0)[:PAGE]
        inside = lax.broadcasted_iota(jnp.int32, page.shape, 0)
        out_ref[i] = jnp.where(inside < count_ref[base + i], page, 0.0).astype(jnp.bfloat16)
        return carry

    lax.fori_loop(0, group, fill, 0)


def fill_pages(pieces, start, count, at):
    slots, width = start.shape[0], pieces[0].shape[1]
    total = sum(piece.shape[0] for piece in pieces)
    return pl.pallas_call(
        pages_kernel,
        grid_spec=pltpu.PrefetchScalarGridSpec(
            num_scalar_prefetch=3,
            grid=(slots // SLOT_GROUP,),
            in_specs=[pl.BlockSpec(piece.shape, lambda i, *_: (0, 0)) for piece in pieces],
            out_specs=pl.BlockSpec((SLOT_GROUP, PAGE, width), lambda i, *_: (i, 0, 0)),
            scratch_shapes=[pltpu.VMEM((total + PAGE, width), jnp.float32)],
        ),
        out_shape=jax.ShapeDtypeStruct((slots, PAGE, width), jnp.bfloat16),
        cost_estimate=SMALL,
        name="fill_pages",
    )(at, start, count, *pieces)


def page_sources(prompt_lengths, starts, request_prompt, page_table, slots):
    pages_per = page_table.shape[1]
    slot_ids = lax.axis_index("dp") * slots + jnp.arange(slots, dtype=jnp.int32)
    flat_table = page_table.reshape(-1)
    matches = slot_ids[:, None] == flat_table[None, :]
    is_used = jnp.any(matches, axis=1)
    entry_ids = jnp.sum(
        jnp.where(matches, jnp.arange(flat_table.shape[0], dtype=jnp.int32)[None, :], 0), axis=1
    )
    request_ids = entry_ids // pages_per
    offset = (entry_ids % pages_per) * PAGE
    request_match = (
        request_ids[:, None] == jnp.arange(request_prompt.shape[0], dtype=jnp.int32)[None, :]
    )
    prompt_pick = jnp.sum(jnp.where(request_match, request_prompt[None, :], 0), axis=1)
    prompt_match = (
        prompt_pick[:, None] == jnp.arange(prompt_lengths.shape[0], dtype=jnp.int32)[None, :]
    )
    slot_start = jnp.sum(jnp.where(prompt_match, starts[None, :], 0), axis=1)
    slot_length = jnp.sum(jnp.where(prompt_match, prompt_lengths[None, :], 0), axis=1)
    count = jnp.where(is_used, jnp.clip(slot_length - offset, 0, PAGE), 0)
    return jnp.where(count > 0, slot_start + offset, 0), count


def shards(
    attn_input,
    attn_gain,
    qkv_weight,
    mlp_input,
    mlp_gain,
    gate_up_weight,
    prompt_lengths,
    request_prompt,
    page_table,
):
    model_ways = lax.axis_size("mp")
    quarter_count = model_ways // KVH
    heads_here = HEADS // model_ways
    piece_dim = HD // quarter_count
    tok_here = attn_input.shape[0]
    rows = qkv_weight.shape[0]

    data_at = lax.axis_index("dp")
    at = data_at[None].astype(jnp.int32)
    token_ids = data_at * tok_here + jnp.arange(tok_here, dtype=jnp.int32)
    starts = jnp.cumsum(prompt_lengths) - prompt_lengths
    begun = token_ids[:, None] >= starts[None, :]
    first = jnp.max(jnp.where(begun, starts[None, :], 0), axis=1)

    order = Order()
    held = {}

    def heads_done(near, far):
        held["queries"], kv_local = finish_heads(near, far, token_ids - first)
        held["pieces"] = [kv_local]
        return kv_local

    def spread(bit):
        def step():
            pieces = order.tie(*held["pieces"])
            joined = pieces[0] if bit == 1 else jnp.concatenate(pieces)
            order.done(joined)
            held["pieces"] = [*pieces, swap(joined, "dp", bit)]

        return step

    def attention():
        pieces = order.tie(*held["pieces"])
        held["attended"] = attend(
            held["queries"], pieces, first[:, None], token_ids[:, None], at
        )
        order.done(held["attended"])
        held["pieces"] = pieces

    def paging():
        pieces = order.tie(*held["pieces"])
        if quarter_count > 1:
            piece_at = (lax.axis_index("mp") // KVH) * piece_dim
            pieces = [
                jnp.concatenate(
                    [
                        lax.dynamic_slice_in_dim(piece, side + piece_at, piece_dim, 1)
                        for side in (0, HD)
                    ],
                    axis=1,
                )
                for piece in pieces
            ]
        sources = page_sources(prompt_lengths, starts, request_prompt, page_table, SLOT_DEV)
        held["kv_cache"] = fill_pages(pieces, *sources, at)
        order.done(held["kv_cache"])

    def head_starts(device):
        kv_head, quarter = device % KVH, device // KVH
        query = (kv_head * quarter_count + quarter) * heads_here
        return [*[query + h for h in range(heads_here)], HEADS + kv_head, HEADS + KVH + kv_head]

    model_ways_cols = gate_up_weight.shape[1] // 2 // model_ways
    heads_job = Job(order, (heads_here + 2) * HD, heads_done)
    jobs = [heads_job, *feed_forward_jobs(order, model_ways_cols, heads_job.width)]
    near, far = pack_heads(qkv_weight, head_starts)
    order.done(near)
    heads_job.stored = (near, swap(far, "mp", 1))
    first_jobs, last_jobs = jobs[2:], []
    while first_jobs and first_jobs[-1].width != jobs[1].width:
        last_jobs = [first_jobs.pop(), *last_jobs]
    store_feed_forward(order, jobs[1:2], gate_up_weight, model_ways_cols)
    tokens = Tokens(order, (attn_input, mlp_input), (attn_gain, mlp_gain), rows)
    heads_job.send_weights()
    jobs[1].send_weights()
    if first_jobs:
        store_feed_forward(order, first_jobs, gate_up_weight, model_ways_cols)
    heads_job.join_weights()
    heads_job.blocks, mlp_blocks = tokens.blocks()
    for job in jobs[1:]:
        job.blocks = mlp_blocks

    def store_last():
        if last_jobs:
            store_feed_forward(order, last_jobs, gate_up_weight, model_ways_cols)

    levels = len(heads_job.bits)
    final = len(jobs) + levels
    early = {}
    for i, bit in enumerate(heads_job.bits):
        early.setdefault(min(levels + 2 + i, final), []).append(spread(bit))
    late = {min(2 * levels + 1, final): [attention, paging]}
    run_jobs(jobs, last_jobs, store_last, early, late)
    hidden = jnp.concatenate([job.result for job in jobs[1:]], axis=1)
    return (held["attended"], hidden, held["kv_cache"])


def solution(mesh):
    data_ways = mesh.shape["dp"]
    placed = (
        P("dp", None),
        P(),
        P(("dp", "mp"), None),
        P("dp", None),
        P(),
        P(("dp", "mp"), None),
        P(),
        P(),
        P(),
    )

    def run(*args):
        return jax.shard_map(
            shards,
            mesh=mesh,
            in_specs=placed,
            out_specs=(P("dp", "mp"), P("dp", "mp"), P("dp", None, "mp")),
            check_vma=False,
        )(*args)

    return run
```

profile of v0, /device:TPU:0, one launch (start us, length us, event | category | flops | bytes accessed | tf_op | source)
XLA Modules:
  0.0 283.8 jit_solution(3524795490667003369)
XLA Ops:
  0.6 3.5 %pack_heads.1 = (bf16[2,160,1536]{2,1,0:T(8,128)(2,1)}, bf16[2,160,1536]{2,1,0:T(8,128)(2,1)}) custom-call(s32[1]{0:T(128)} %bitcast.3.at_ref, f32[160,6144]{1,0:T(8,128)} %refs_11_.1, f32[160,6144]{1,0:T(8,128)} %refs_11_.1, f32[160,6144]{1,0:T(8,128)} %refs_11_.1, f32[160,6144]{1,0:T(8,128)} %refs_11_.1, f32[160,6144]{1,0:T(8,128)} %refs_11_.1, ...), custom_call_target="tpu_custom_call" | custom-call | flops 1 | bytes 1 | tf_op jit(solution)/shard_map/pack_heads/pallas_call | solution.py:192
  4.7 4.4 %pack_columns.3 = (bf16[2,160,1536]{2,1,0:T(8,128)(2,1)}, bf16[2,160,1536]{2,1,0:T(8,128)(2,1)}) custom-call(s32[1]{0:T(128)} %bitcast.3.at_ref, f32[160,32768]{1,0:T(8,128)} %refs_3_.4, f32[160,32768]{1,0:T(8,128)} %refs_3_.4, f32[160,32768]{1,0:T(8,128)} %refs_3_.4, f32[160,32768]{1,0:T(8,128)} %refs_3_.4), custom_call_target="tpu_custom_call" | custom-call | flops 1 | bytes 1 | tf_op jit(solution)/shard_map/pack_columns/pallas_call | solution.py:154
  9.8 9.3 %token_cells.1 = (bf16[256,640]{1,0:T(8,128)(2,1)}, bf16[256,640]{1,0:T(8,128)(2,1)}, bf16[2,256,640]{2,1,0:T(8,128)(2,1)}, bf16[2,256,640]{2,1,0:T(8,128)(2,1)}, bf16[2,256,640]{2,1,0:T(8,128)(2,1)}) custom-call(s32[3]{0:T(128)} %pad_add_fusion.at_ref, bf16[256,5120]{1,0:T(8,128)(2,1)} %refs_0_.3, bf16[256,5120]{1,0:T(8,128)(2,1)} %refs_1_.3, ...), custom_call_target="tpu_custom_call" | custom-call | flops 1 | bytes 1 | tf_op jit(solution)/shard_map/token_cells/pallas_call | solution.py:99
  19.0 2.9 %collective-permute-start.3 = (bf16[2,256,640]{2,1,0:T(8,128)(2,1)}, bf16[2,256,640]{2,1,0:T(8,128)(2,1)S(1)}, u32[]{:S(2)}, u32[]{:S(2)}) collective-permute-start(bf16[2,256,640]{2,1,0:T(8,128)(2,1)} %get-tuple-element.140), channel_id=1, source_target_pairs={{0,8},{8,0},{16,24},{24,16},{1,9},{9,1},{17,25},{25,17},{2,10},{10... | collective-permute-start | bytes 1966088 | tf_op jit(solution)/shard_map/ppermute | solution.py:30
  22.0 1.5 collective-permute-start.4
  30.4 2.1 collective-permute-start.1
  34.8 13.4 %pack_columns.4 = (bf16[2,160,6144]{2,1,0:T(8,128)(2,1)}, bf16[2,160,6144]{2,1,0:T(8,128)(2,1)}) custom-call(s32[1]{0:T(128)} %bitcast.3.at_ref, f32[160,32768]{1,0:T(8,128)} %refs_3_.4, f32[160,32768]{1,0:T(8,128)} %refs_3_.4, f32[160,32768]{1,0:T(8,128)} %refs_3_.4, f32[160,32768]{1,0:T(8,128)} %refs_3_.4), custom_call_target="tpu_custom_call" | custom-call | flops 1 | bytes 1 | tf_op jit(solution)/shard_map/pack_columns/pallas_call | solution.py:154
  49.9 4.0 %collective-permute-done.1 = bf16[2,160,1536]{2,1,0:T(8,128)(2,1)} collective-permute-done((bf16[2,160,1536]{2,1,0:T(8,128)(2,1)}, bf16[2,160,1536]{2,1,0:T(8,128)(2,1)}, u32[]{:S(2)}, u32[]{:S(2)}) %collective-permute-start.1) | collective-permute-done | bytes 983072 | tf_op jit(solution)/shard_map/ppermute | solution.py:30
  53.9 1.7 collective-permute-start.8
  57.1 2.1 slice_bitcast_fusion.25
  60.0 1.7 convolution_convert_fusion.11
  62.5 1.7 convolution_convert_fusion.10
  64.2 1.5 collective-permute-start.6
  65.7 1.5 collective-permute-start.7
  67.2 1.4 fusion.34
  68.5 1.4 fusion.15
  70.5 1.4 fusion.69
  71.8 2.0 copy-done.2
  76.6 3.5 %pack_columns.5 = (bf16[2,160,512]{2,1,0:T(8,128)(2,1)}, bf16[2,160,512]{2,1,0:T(8,128)(2,1)}) custom-call(s32[1]{0:T(128)} %bitcast.3.at_ref, f32[160,32768]{1,0:T(8,128)} %refs_3_.4, f32[160,32768]{1,0:T(8,128)} %refs_3_.4, f32[160,32768]{1,0:T(8,128)} %refs_3_.4, f32[160,32768]{1,0:T(8,128)} %refs_3_.4), custom_call_target="tpu_custom_call" | custom-call | flops 1 | bytes 1 | tf_op jit(solution)/shard_map/pack_columns/pallas_call | solution.py:154
  80.2 1.7 collective-permute-done.10
  81.9 1.4 slice_bitcast_fusion.18
  89.2 1.4 add_convert_fusion.16
  91.1 1.6 copy-done.1
  92.9 1.6 collective-permute-start.17
  94.7 1.4 fusion.33
  97.9 1.7 collective-permute-done.13
  101.1 1.4 fusion.32
  104.2 12.5 %collective-permute-done.11 = bf16[768,768]{1,0:T(8,128)(2,1)S(1)} collective-permute-done((bf16[768,768]{1,0:T(8,128)(2,1)S(1)}, bf16[768,768]{1,0:T(8,128)(2,1)S(1)}, u32[]{:S(2)}, u32[]{:S(2)}) %collective-permute-start.11) | collective-permute-done | bytes 1179680 | tf_op jit(solution)/shard_map/ppermute | solution.py:30
  116.7 1.6 collective-permute-done.12
  118.5 1.4 collective-permute-start.15
  121.8 2.7 collective-permute-start.14
  125.7 1.6 collective-permute-start.18
  128.2 1.4 fusion.26
  131.4 1.4 fusion.31
  134.5 10.8 %collective-permute-done.15 = bf16[768,768]{1,0:T(8,128)(2,1)S(1)} collective-permute-done((bf16[768,768]{1,0:T(8,128)(2,1)S(1)}, bf16[768,768]{1,0:T(8,128)(2,1)S(1)}, u32[]{:S(2)}, u32[]{:S(2)}) %collective-permute-start.15) | collective-permute-done | bytes 1179680 | tf_op jit(solution)/shard_map/ppermute | solution.py:30
  145.3 1.5 collective-permute-done.16
  150.2 2.1 convert_add_fusion.5.near_ref
  152.4 2.3 finish_heads.1
  154.7 1.5 add_convert_fusion.10
  156.1 2.8 collective-permute-start.21
  161.5 1.6 collective-permute-start.20
  165.3 1.5 collective-permute-start.19
  168.9 1.4 fusion.30
  171.5 1.4 fusion.73
  174.1 2.6 collective-permute-done.23
  178.0 1.8 collective-permute-start.26
  184.0 2.7 collective-permute-start.25
  187.6 11.3 %collective-permute-done.20 = bf16[2,160,1536]{2,1,0:T(8,128)(2,1)S(1)} collective-permute-done((bf16[2,160,1536]{2,1,0:T(8,128)(2,1)S(1)}, bf16[2,160,1536]{2,1,0:T(8,128)(2,1)S(1)}, u32[]{:S(2)}, u32[]{:S(2)}) %collective-permute-start.20) | collective-permute-done | bytes 983072 | tf_op jit(solution)/shard_map/ppermute | solution.py:30
  200.6 1.4 fusion.24
  205.3 1.4 fusion.74
  208.1 1.9 collective-permute-start.29
  211.2 1.6 collective-permute-start.30
  212.9 1.9 add_convert_fusion.4
  217.9 5.7 %attend.1 = bf16[256,512]{1,0:T(8,128)(2,1)} custom-call(s32[1]{0:T(128)} %bitcast.at_ref, bf16[256,512]{1,0:T(8,128)(2,1)} %get-tuple-element.182.q_ref, s32[256,1]{1,0:T(8,128)} %copy.14.first_ref, s32[256,1]{1,0:T(8,128)} %iota_add_fusion.token_ref, bf16[256,256]{1,0:T(8,128)(2,1)} %get-tuple-element.218.refs_0_, bf16[256,256]{1,0:T(8,128)(2,1)} %copy-done.9, ...), custom_call_target="tpu_custom_call" | custom-call | flops 1 | bytes 1 | tf_op jit(solution)/shard_map/attend/pallas_call | solution.py:457
  223.6 10.4 %fill_pages.1 = bf16[96,128,256]{2,1,0:T(8,128)(2,1)} custom-call(s32[1]{0:T(128)} %bitcast.at_ref, s32[96]{0:T(128)} %get-tuple-element.255.start_ref, s32[96]{0:T(128)} %get-tuple-element.256.count_ref, bf16[256,256]{1,0:T(8,128)(2,1)} %get-tuple-element.218.refs_0_, bf16[256,256]{1,0:T(8,128)(2,1)} %copy-done.9, ...), custom_call_target="tpu_custom_call" | custom-call | flops 1 | bytes 1 | tf_op jit(solution)/shard_map/fill_pages/pallas_call | solution.py:504
  241.2 1.5 collective-permute-start.35
  243.8 1.7 collective-permute-start.36
  246.6 2.3 collective-permute-start.32
  251.7 1.4 collective-permute-done.36
  253.8 1.6 collective-permute-start.39
  256.4 2.2 collective-permute-start.37
  258.7 14.9 %collective-permute-done.32 = bf16[256,768]{1,0:T(8,128)(2,1)S(1)} collective-permute-done((bf16[256,768]{1,0:T(8,128)(2,1)S(1)}, bf16[256,768]{1,0:T(8,128)(2,1)S(1)}, u32[]{:S(2)}, u32[]{:S(2)}) %collective-permute-start.32) | collective-permute-done | bytes 393248 | tf_op jit(solution)/shard_map/ppermute | solution.py:30
  275.8 3.3 %collective-permute-done.37 = bf16[256,768]{1,0:T(8,128)(2,1)S(1)} collective-permute-done((bf16[256,768]{1,0:T(8,128)(2,1)S(1)}, bf16[256,768]{1,0:T(8,128)(2,1)S(1)}, u32[]{:S(2)}, u32[]{:S(2)}) %collective-permute-start.37) | collective-permute-done | bytes 393248 | tf_op jit(solution)/shard_map/ppermute | solution.py:30
  281.1 2.0 collective-permute-done.40
  (320 shorter events, 85.9 us)
Async XLA Ops:
  4.2 23.9 %collective-permute-start = (bf16[2,160,1536]{2,1,0:T(8,128)(2,1)}, bf16[2,160,1536]{2,1,0:T(8,128)(2,1)}, u32[]{:S(2)}, u32[]{:S(2)}) collective-permute-start(bf16[2,160,1536]{2,1,0:T(8,128)(2,1)} %get-tuple-element.131), channel_id=1, source_target_pairs={{0,1},{1,0},{2,3},{3,2},{4,5},{5,4},{6,7},{7,6},{8,9},{9,8},{10,11... | collective-permute-start | bytes 2949128 | tf_op jit(solution)/shard_map/ppermute | solution.py:30
  9.0 23.4 %collective-permute-start.2 = (bf16[2,160,1536]{2,1,0:T(8,128)(2,1)}, bf16[2,160,1536]{2,1,0:T(8,128)(2,1)}, u32[]{:S(2)}, u32[]{:S(2)}) collective-permute-start(bf16[2,160,1536]{2,1,0:T(8,128)(2,1)} %get-tuple-element.134), channel_id=1, source_target_pairs={{0,1},{1,0},{2,3},{3,2},{4,5},{5,4},{6,7},{7,6},{8,9},{9,8},{10,11... | collective-permute-start | bytes 2949128 | tf_op jit(solution)/shard_map/ppermute | solution.py:30
  9.7 13.8 %copy-start.58 = (s32[64,4]{0,1:T(4,128)S(1)}, s32[64,4]{0,1:T(4,128)}, u32[]{:S(2)}) copy-start(s32[64,4]{0,1:T(4,128)} %param.17) | copy-start | bytes 3076
  9.7 14.3 %copy-start.59 = (s32[6]{0:T(128)S(1)}, s32[6]{0:T(128)}, u32[]{:S(2)}) copy-start(s32[6]{0:T(128)} %param.15) | copy-start | bytes 76
  9.8 15.4 %copy-start.60 = (s32[64]{0:T(128)S(1)}, s32[64]{0:T(128)}, u32[]{:S(2)}) copy-start(s32[64]{0:T(128)} %param.16) | copy-start | bytes 772
  19.0 9.0 %copy-start.23 = (bf16[2,160,1536]{2,1,0:T(8,128)(2,1)S(1)}, bf16[2,160,1536]{2,1,0:T(8,128)(2,1)}, u32[]{:S(2)}) copy-start(bf16[2,160,1536]{2,1,0:T(8,128)(2,1)} %get-tuple-element.132) | copy-start | bytes 2949124
  19.0 38.1 %collective-permute-start.3 = (bf16[2,256,640]{2,1,0:T(8,128)(2,1)}, bf16[2,256,640]{2,1,0:T(8,128)(2,1)S(1)}, u32[]{:S(2)}, u32[]{:S(2)}) collective-permute-start(bf16[2,256,640]{2,1,0:T(8,128)(2,1)} %get-tuple-element.140), channel_id=1, source_target_pairs={{0,8},{8,0},{16,24},{24,16},{1,9},{9,1},{17,25},{25,17},{2,10},{10... | collective-permute-start | bytes 1966088 | tf_op jit(solution)/shard_map/ppermute | solution.py:30
  22.0 35.2 %collective-permute-start.4 = (bf16[2,256,640]{2,1,0:T(8,128)(2,1)}, bf16[2,256,640]{2,1,0:T(8,128)(2,1)S(1)}, u32[]{:S(2)}, u32[]{:S(2)}) collective-permute-start(bf16[2,256,640]{2,1,0:T(8,128)(2,1)} %get-tuple-element.141), channel_id=1, source_target_pairs={{0,16},{8,24},{16,0},{24,8},{1,17},{9,25},{17,1},{25,9},{2,18},{10... | collective-permute-start | bytes 1966088 | tf_op jit(solution)/shard_map/ppermute | solution.py:30
  23.5 33.6 %collective-permute-start.5 = (bf16[2,256,640]{2,1,0:T(8,128)(2,1)}, bf16[2,256,640]{2,1,0:T(8,128)(2,1)}, u32[]{:S(2)}, u32[]{:S(2)}) collective-permute-start(bf16[2,256,640]{2,1,0:T(8,128)(2,1)} %get-tuple-element.142), channel_id=1, source_target_pairs={{0,24},{8,16},{16,8},{24,0},{1,25},{9,17},{17,9},{25,1},{2,26},{10... | collective-permute-start | bytes 1966088 | tf_op jit(solution)/shard_map/ppermute | solution.py:30
  29.3 4.3 %copy-start.18 = (bf16[2,160,1536]{2,1,0:T(8,128)(2,1)S(1)}, bf16[2,160,1536]{2,1,0:T(8,128)(2,1)}, u32[]{:S(2)}) copy-start(bf16[2,160,1536]{2,1,0:T(8,128)(2,1)} %get-tuple-element.135) | copy-start | bytes 2949124
  30.4 23.6 %collective-permute-start.1 = (bf16[2,160,1536]{2,1,0:T(8,128)(2,1)}, bf16[2,160,1536]{2,1,0:T(8,128)(2,1)}, u32[]{:S(2)}, u32[]{:S(2)}) collective-permute-start(bf16[2,160,1536]{2,1,0:T(8,128)(2,1)} %pad_maximum_fusion.10), channel_id=1, source_target_pairs={{0,2},{1,3},{2,0},{3,1},{4,6},{5,7},{6,4},{7,5},{8,10},{9,11},{10,... | collective-permute-start | bytes 2949128 | tf_op jit(solution)/shard_map/ppermute | solution.py:30
  48.2 23.6 %collective-permute-start.9 = (bf16[2,160,6144]{2,1,0:T(8,128)(2,1)}, bf16[2,160,6144]{2,1,0:T(8,128)(2,1)S(1)}, u32[]{:S(2)}, u32[]{:S(2)}) collective-permute-start(bf16[2,160,6144]{2,1,0:T(8,128)(2,1)} %get-tuple-element.148), channel_id=1, source_target_pairs={{0,1},{1,0},{2,3},{3,2},{4,5},{5,4},{6,7},{7,6},{8,9},{9,8},{10,11... | collective-permute-start | bytes 11796488 | tf_op jit(solution)/shard_map/ppermute | solution.py:30
  53.9 26.2 %collective-permute-start.8 = (bf16[2,160,1536]{2,1,0:T(8,128)(2,1)}, bf16[2,160,1536]{2,1,0:T(8,128)(2,1)}, u32[]{:S(2)}, u32[]{:S(2)}) collective-permute-start(bf16[2,160,1536]{2,1,0:T(8,128)(2,1)} %pad_maximum_fusion.11), channel_id=1, source_target_pairs={{0,2},{1,3},{2,0},{3,1},{4,6},{5,7},{6,4},{7,5},{8,10},{9,11},{10,... | collective-permute-start | bytes 2949128 | tf_op jit(solution)/shard_map/ppermute | solution.py:30
  57.1 11.4 %copy-start.32 = (bf16[2,256,640]{2,1,0:T(8,128)(2,1)}, bf16[2,256,640]{2,1,0:T(8,128)(2,1)S(1)}, u32[]{:S(2)}) copy-start(bf16[2,256,640]{2,1,0:T(8,128)(2,1)S(1)} %collective-permute-done.3) | copy-start | bytes 1966084
  61.7 5.5 %copy-start.49 = (bf16[256,640]{1,0:T(8,128)(2,1)S(1)}, bf16[256,640]{1,0:T(8,128)(2,1)}, u32[]{:S(2)}) copy-start(bf16[256,640]{1,0:T(8,128)(2,1)} %get-tuple-element.130) | copy-start | bytes 983044
  64.2 23.2 %collective-permute-start.6 = (bf16[512,768]{1,0:T(8,128)(2,1)}, bf16[512,768]{1,0:T(8,128)(2,1)}, u32[]{:S(2)}, u32[]{:S(2)}) collective-permute-start(bf16[512,768]{1,0:T(8,128)(2,1)} %convolution_convert_fusion.11), channel_id=1, source_target_pairs={{0,16},{8,24},{16,0},{24,8},{1,17},{9,25},{17,1},{25,9},{2,18},{10... | collective-permute-start | bytes 2359304 | tf_op jit(solution)/shard_map/ppermute | solution.py:30
  65.7 21.7 %collective-permute-start.7 = (bf16[512,768]{1,0:T(8,128)(2,1)}, bf16[512,768]{1,0:T(8,128)(2,1)}, u32[]{:S(2)}, u32[]{:S(2)}) collective-permute-start(bf16[512,768]{1,0:T(8,128)(2,1)} %convolution_convert_fusion.10), channel_id=1, source_target_pairs={{0,8},{8,0},{16,24},{24,16},{1,9},{9,1},{17,25},{25,17},{2,10},{10... | collective-permute-start | bytes 2359304 | tf_op jit(solution)/shard_map/ppermute | solution.py:30
  76.1 23.5 %collective-permute-start.13 = (bf16[2,160,1536]{2,1,0:T(8,128)(2,1)}, bf16[2,160,1536]{2,1,0:T(8,128)(2,1)S(1)}, u32[]{:S(2)}, u32[]{:S(2)}) collective-permute-start(bf16[2,160,1536]{2,1,0:T(8,128)(2,1)} %pad_maximum_fusion.14), channel_id=1, source_target_pairs={{0,2},{1,3},{2,0},{3,1},{4,6},{5,7},{6,4},{7,5},{8,10},{9,11},{10,... | collective-permute-start | bytes 2949128 | tf_op jit(solution)/shard_map/ppermute | solution.py:30
  80.1 1.8 collective-permute-start.10
  88.6 28.1 %collective-permute-start.11 = (bf16[768,768]{1,0:T(8,128)(2,1)S(1)}, bf16[768,768]{1,0:T(8,128)(2,1)S(1)}, u32[]{:S(2)}, u32[]{:S(2)}) collective-permute-start(bf16[768,768]{1,0:T(8,128)(2,1)S(1)} %pad_maximum_fusion), channel_id=1, source_target_pairs={{0,16},{8,24},{16,0},{24,8},{1,17},{9,25},{17,1},{25,9},{2,18},{10... | collective-permute-start | bytes 3538952 | tf_op jit(solution)/shard_map/ppermute | solution.py:30
  90.7 27.7 %collective-permute-start.12 = (bf16[768,768]{1,0:T(8,128)(2,1)S(1)}, bf16[768,768]{1,0:T(8,128)(2,1)S(1)}, u32[]{:S(2)}, u32[]{:S(2)}) collective-permute-start(bf16[768,768]{1,0:T(8,128)(2,1)S(1)} %pad_maximum_fusion.1), channel_id=1, source_target_pairs={{0,8},{8,0},{16,24},{24,16},{1,9},{9,1},{17,25},{25,17},{2,10},{10... | collective-permute-start | bytes 3538952 | tf_op jit(solution)/shard_map/ppermute | solution.py:30
  92.9 34.3 %collective-permute-start.17 = (bf16[2,160,1536]{2,1,0:T(8,128)(2,1)S(1)}, bf16[2,160,1536]{2,1,0:T(8,128)(2,1)S(1)}, u32[]{:S(2)}, u32[]{:S(2)}) collective-permute-start(bf16[2,160,1536]{2,1,0:T(8,128)(2,1)S(1)} %pad_maximum_fusion.17), channel_id=1, source_target_pairs={{0,2},{1,3},{2,0},{3,1},{4,6},{5,7},{6,4},{7,5},{8,10},{9,11},{10,... | collective-permute-start | bytes 2949128 | tf_op jit(solution)/shard_map/ppermute | solution.py:30
  116.7 33.5 %copy-start.10 = (bf16[768,768]{1,0:T(8,128)(2,1)}, bf16[768,768]{1,0:T(8,128)(2,1)S(1)}, u32[]{:S(2)}) copy-start(bf16[768,768]{1,0:T(8,128)(2,1)S(1)} %collective-permute-done.11) | copy-start | bytes 3538948
  118.5 26.8 %collective-permute-start.15 = (bf16[768,768]{1,0:T(8,128)(2,1)S(1)}, bf16[768,768]{1,0:T(8,128)(2,1)S(1)}, u32[]{:S(2)}, u32[]{:S(2)}) collective-permute-start(bf16[768,768]{1,0:T(8,128)(2,1)S(1)} %pad_maximum_fusion.2), channel_id=1, source_target_pairs={{0,16},{8,24},{16,0},{24,8},{1,17},{9,25},{17,1},{25,9},{2,18},{10... | collective-permute-start | bytes 3538952 | tf_op jit(solution)/shard_map/ppermute | solution.py:30
  120.1 26.6 %collective-permute-start.16 = (bf16[768,768]{1,0:T(8,128)(2,1)S(1)}, bf16[768,768]{1,0:T(8,128)(2,1)S(1)}, u32[]{:S(2)}, u32[]{:S(2)}) collective-permute-start(bf16[768,768]{1,0:T(8,128)(2,1)S(1)} %pad_maximum_fusion.3), channel_id=1, source_target_pairs={{0,8},{8,0},{16,24},{24,16},{1,9},{9,1},{17,25},{25,17},{2,10},{10... | collective-permute-start | bytes 3538952 | tf_op jit(solution)/shard_map/ppermute | solution.py:30
  121.8 28.4 %collective-permute-start.14 = (bf16[256,768]{1,0:T(8,128)(2,1)S(1)}, bf16[256,768]{1,0:T(8,128)(2,1)S(1)}, u32[]{:S(2)}, u32[]{:S(2)}) collective-permute-start(bf16[256,768]{1,0:T(8,128)(2,1)S(1)} %add_convert_fusion.13), channel_id=1, source_target_pairs={{0,4},{1,5},{2,6},{3,7},{4,0},{5,1},{6,2},{7,3},{8,12},{9,13},{10,... | collective-permute-start | bytes 1179656 | tf_op jit(solution)/shard_map/ppermute | solution.py:30
  125.7 37.5 %collective-permute-start.18 = (bf16[2,160,1536]{2,1,0:T(8,128)(2,1)}, bf16[2,160,1536]{2,1,0:T(8,128)(2,1)}, u32[]{:S(2)}, u32[]{:S(2)}) collective-permute-start(bf16[2,160,1536]{2,1,0:T(8,128)(2,1)} %pad_maximum_fusion.20), channel_id=1, source_target_pairs={{0,2},{1,3},{2,0},{3,1},{4,6},{5,7},{6,4},{7,5},{8,10},{9,11},{10,... | collective-permute-start | bytes 2949128 | tf_op jit(solution)/shard_map/ppermute | solution.py:30
  145.3 3.4 %copy-start.16 = (bf16[768,768]{1,0:T(8,128)(2,1)}, bf16[768,768]{1,0:T(8,128)(2,1)S(1)}, u32[]{:S(2)}) copy-start(bf16[768,768]{1,0:T(8,128)(2,1)S(1)} %collective-permute-done.15) | copy-start | bytes 3538948
  148.1 26.1 %collective-permute-start.22 = (bf16[768,768]{1,0:T(8,128)(2,1)}, bf16[768,768]{1,0:T(8,128)(2,1)}, u32[]{:S(2)}, u32[]{:S(2)}) collective-permute-start(bf16[768,768]{1,0:T(8,128)(2,1)} %pad_maximum_fusion.4), channel_id=1, source_target_pairs={{0,16},{8,24},{16,0},{24,8},{1,17},{9,25},{17,1},{25,9},{2,18},{10... | collective-permute-start | bytes 3538952 | tf_op jit(solution)/shard_map/ppermute | solution.py:30
  149.8 27.0 %collective-permute-start.23 = (bf16[768,768]{1,0:T(8,128)(2,1)}, bf16[768,768]{1,0:T(8,128)(2,1)}, u32[]{:S(2)}, u32[]{:S(2)}) collective-permute-start(bf16[768,768]{1,0:T(8,128)(2,1)} %pad_maximum_fusion.5), channel_id=1, source_target_pairs={{0,8},{8,0},{16,24},{24,16},{1,9},{9,1},{17,25},{25,17},{2,10},{10... | collective-permute-start | bytes 3538952 | tf_op jit(solution)/shard_map/ppermute | solution.py:30
  156.1 25.4 %collective-permute-start.21 = (bf16[256,768]{1,0:T(8,128)(2,1)S(1)}, bf16[256,768]{1,0:T(8,128)(2,1)S(1)}, u32[]{:S(2)}, u32[]{:S(2)}) collective-permute-start(bf16[256,768]{1,0:T(8,128)(2,1)S(1)} %add_convert_fusion.10), channel_id=1, source_target_pairs={{0,4},{1,5},{2,6},{3,7},{4,0},{5,1},{6,2},{7,3},{8,12},{9,13},{10,... | collective-permute-start | bytes 1179656 | tf_op jit(solution)/shard_map/ppermute | solution.py:30
  161.5 37.3 %collective-permute-start.20 = (bf16[2,160,1536]{2,1,0:T(8,128)(2,1)S(1)}, bf16[2,160,1536]{2,1,0:T(8,128)(2,1)S(1)}, u32[]{:S(2)}, u32[]{:S(2)}) collective-permute-start(bf16[2,160,1536]{2,1,0:T(8,128)(2,1)S(1)} %pad_maximum_fusion.23), channel_id=1, source_target_pairs={{0,2},{1,3},{2,0},{3,1},{4,6},{5,7},{6,4},{7,5},{8,10},{9,11},{10,... | collective-permute-start | bytes 2949128 | tf_op jit(solution)/shard_map/ppermute | solution.py:30
  165.3 33.7 %collective-permute-start.19 = (bf16[256,256]{1,0:T(8,128)(2,1)S(1)}, bf16[256,256]{1,0:T(8,128)(2,1)S(1)}, u32[]{:S(2)}, u32[]{:S(2)}) collective-permute-start(bf16[256,256]{1,0:T(8,128)(2,1)S(1)} %copy-done.8), channel_id=1, source_target_pairs={{0,8},{8,0},{16,24},{24,16},{1,9},{9,1},{17,25},{25,17},{2,10},{10... | collective-permute-start | bytes 393224 | tf_op jit(solution)/shard_map/ppermute | solution.py:30
  172.9 6.8 %copy-start.24 = (f32[256,768]{1,0:T(8,128)S(1)}, f32[256,768]{1,0:T(8,128)}, u32[]{:S(2)}) copy-start(f32[256,768]{1,0:T(8,128)} %fusion.26) | copy-start | bytes 2359300
  177.9 3.6 %copy-start.6 = (f32[256,768]{1,0:T(8,128)S(1)}, f32[256,768]{1,0:T(8,128)}, u32[]{:S(2)}) copy-start(f32[256,768]{1,0:T(8,128)} %fusion.70) | copy-start | bytes 2359300
  177.9 3.6 %copy-start.17 = (bf16[768,768]{1,0:T(8,128)(2,1)S(1)}, bf16[768,768]{1,0:T(8,128)(2,1)}, u32[]{:S(2)}) copy-start(bf16[768,768]{1,0:T(8,128)(2,1)} %copy-done.16) | copy-start | bytes 3538948
  178.0 28.8 %collective-permute-start.26 = (bf16[768,768]{1,0:T(8,128)(2,1)S(1)}, bf16[768,768]{1,0:T(8,128)(2,1)S(1)}, u32[]{:S(2)}, u32[]{:S(2)}) collective-permute-start(bf16[768,768]{1,0:T(8,128)(2,1)S(1)} %pad_maximum_fusion.6), channel_id=1, source_target_pairs={{0,16},{8,24},{16,0},{24,8},{1,17},{9,25},{17,1},{25,9},{2,18},{10... | collective-permute-start | bytes 3538952 | tf_op jit(solution)/shard_map/ppermute | solution.py:30
  180.9 25.8 %collective-permute-start.27 = (bf16[768,768]{1,0:T(8,128)(2,1)S(1)}, bf16[768,768]{1,0:T(8,128)(2,1)S(1)}, u32[]{:S(2)}, u32[]{:S(2)}) collective-permute-start(bf16[768,768]{1,0:T(8,128)(2,1)S(1)} %pad_maximum_fusion.7), channel_id=1, source_target_pairs={{0,8},{8,0},{16,24},{24,16},{1,9},{9,1},{17,25},{25,17},{2,10},{10... | collective-permute-start | bytes 3538952 | tf_op jit(solution)/shard_map/ppermute | solution.py:30
  182.7 4.0 %copy-start.48 = (bf16[2,160,512]{2,1,0:T(8,128)(2,1)S(1)}, bf16[2,160,512]{2,1,0:T(8,128)(2,1)}, u32[]{:S(2)}) copy-start(bf16[2,160,512]{2,1,0:T(8,128)(2,1)} %copy-done.47) | copy-start | bytes 983044
  182.7 4.0 %copy-start.46 = (bf16[2,160,512]{2,1,0:T(8,128)(2,1)S(1)}, bf16[2,160,512]{2,1,0:T(8,128)(2,1)}, u32[]{:S(2)}) copy-start(bf16[2,160,512]{2,1,0:T(8,128)(2,1)} %get-tuple-element.201) | copy-start | bytes 983044
  184.0 30.7 %collective-permute-start.25 = (bf16[256,768]{1,0:T(8,128)(2,1)S(1)}, bf16[256,768]{1,0:T(8,128)(2,1)S(1)}, u32[]{:S(2)}, u32[]{:S(2)}) collective-permute-start(bf16[256,768]{1,0:T(8,128)(2,1)S(1)} %add_convert_fusion.7), channel_id=1, source_target_pairs={{0,4},{1,5},{2,6},{3,7},{4,0},{5,1},{6,2},{7,3},{8,12},{9,13},{10,... | collective-permute-start | bytes 1179656 | tf_op jit(solution)/shard_map/ppermute | solution.py:30
  198.8 35.2 %collective-permute-start.31 = (bf16[2,160,512]{2,1,0:T(8,128)(2,1)}, bf16[2,160,512]{2,1,0:T(8,128)(2,1)}, u32[]{:S(2)}, u32[]{:S(2)}) collective-permute-start(bf16[2,160,512]{2,1,0:T(8,128)(2,1)} %pad_maximum_fusion.34), channel_id=1, source_target_pairs={{0,2},{1,3},{2,0},{3,1},{4,6},{5,7},{6,4},{7,5},{8,10},{9,11},{10,... | collective-permute-start | bytes 983048 | tf_op jit(solution)/shard_map/ppermute | solution.py:30
  199.1 17.8 %collective-permute-start.24 = (bf16[512,256]{1,0:T(8,128)(2,1)S(1)}, bf16[512,256]{1,0:T(8,128)(2,1)}, u32[]{:S(2)}, u32[]{:S(2)}) collective-permute-start(bf16[512,256]{1,0:T(8,128)(2,1)S(1)} %constant_dynamic-update-slice_fusion), channel_id=1, source_target_pairs={{0,16},{8,24},{16,0},{24,8},{1,17},{9,25},{17,1},{25,9},{2,18},{10... | collective-permute-start | bytes 786440 | tf_op jit(solution)/shard_map/ppermute | solution.py:30
  206.7 6.1 %copy-start.13 = (bf16[768,768]{1,0:T(8,128)(2,1)}, bf16[768,768]{1,0:T(8,128)(2,1)S(1)}, u32[]{:S(2)}) copy-start(bf16[768,768]{1,0:T(8,128)(2,1)S(1)} %collective-permute-done.27) | copy-start | bytes 3538948
  208.0 4.8 %copy-start.27 = (f32[256,768]{1,0:T(8,128)S(1)}, f32[256,768]{1,0:T(8,128)}, u32[]{:S(2)}) copy-start(f32[256,768]{1,0:T(8,128)} %fusion.31) | copy-start | bytes 2359300
  208.1 31.0 %collective-permute-start.29 = (bf16[768,768]{1,0:T(8,128)(2,1)}, bf16[768,768]{1,0:T(8,128)(2,1)}, u32[]{:S(2)}, u32[]{:S(2)}) collective-permute-start(bf16[768,768]{1,0:T(8,128)(2,1)} %pad_maximum_fusion.8), channel_id=1, source_target_pairs={{0,16},{8,24},{16,0},{24,8},{1,17},{9,25},{17,1},{25,9},{2,18},{10... | collective-permute-start | bytes 3538952 | tf_op jit(solution)/shard_map/ppermute | solution.py:30
  211.2 27.8 %collective-permute-start.30 = (bf16[768,768]{1,0:T(8,128)(2,1)}, bf16[768,768]{1,0:T(8,128)(2,1)}, u32[]{:S(2)}, u32[]{:S(2)}) collective-permute-start(bf16[768,768]{1,0:T(8,128)(2,1)} %pad_maximum_fusion.9), channel_id=1, source_target_pairs={{0,8},{8,0},{16,24},{24,16},{1,9},{9,1},{17,25},{25,17},{2,10},{10... | collective-permute-start | bytes 3538952 | tf_op jit(solution)/shard_map/ppermute | solution.py:30
  214.8 31.8 %collective-permute-start.28 = (bf16[256,768]{1,0:T(8,128)(2,1)}, bf16[256,768]{1,0:T(8,128)(2,1)}, u32[]{:S(2)}, u32[]{:S(2)}) collective-permute-start(bf16[256,768]{1,0:T(8,128)(2,1)} %add_convert_fusion.4), channel_id=1, source_target_pairs={{0,4},{1,5},{2,6},{3,7},{4,0},{5,1},{6,2},{7,3},{8,12},{9,13},{10,... | collective-permute-start | bytes 1179656 | tf_op jit(solution)/shard_map/ppermute | solution.py:30
  223.6 11.5 %copy-start.39 = (bf16[256,640]{1,0:T(8,128)(2,1)S(1)}, bf16[256,640]{1,0:T(8,128)(2,1)}, u32[]{:S(2)}) copy-start(bf16[256,640]{1,0:T(8,128)(2,1)} %get-tuple-element.301) | copy-start | bytes 983044
  223.6 11.5 %copy-start.54 = (bf16[160,256]{1,0:T(8,128)(2,1)S(1)}, bf16[160,256]{1,0:T(8,128)(2,1)}, u32[]{:S(2)}) copy-start(bf16[160,256]{1,0:T(8,128)(2,1)} %get-tuple-element.362) | copy-start | bytes 245764
  238.8 6.7 %copy-start.15 = (bf16[768,768]{1,0:T(8,128)(2,1)S(1)}, bf16[768,768]{1,0:T(8,128)(2,1)}, u32[]{:S(2)}) copy-start(bf16[768,768]{1,0:T(8,128)(2,1)} %copy-done.14) | copy-start | bytes 3538948
  238.8 6.7 %copy-start.28 = (f32[256,768]{1,0:T(8,128)S(1)}, f32[256,768]{1,0:T(8,128)}, u32[]{:S(2)}) copy-start(f32[256,768]{1,0:T(8,128)} %fusion.30) | copy-start | bytes 2359300
  239.1 11.9 %collective-permute-start.33 = (bf16[512,256]{1,0:T(8,128)(2,1)S(1)}, bf16[512,256]{1,0:T(8,128)(2,1)S(1)}, u32[]{:S(2)}, u32[]{:S(2)}) collective-permute-start(bf16[512,256]{1,0:T(8,128)(2,1)S(1)} %convolution_convert_fusion.13), channel_id=1, source_target_pairs={{0,16},{8,24},{16,0},{24,8},{1,17},{9,25},{17,1},{25,9},{2,18},{10... | collective-permute-start | bytes 786440 | tf_op jit(solution)/shard_map/ppermute | solution.py:30
  239.6 11.4 %collective-permute-start.34 = (bf16[512,256]{1,0:T(8,128)(2,1)S(1)}, bf16[512,256]{1,0:T(8,128)(2,1)S(1)}, u32[]{:S(2)}, u32[]{:S(2)}) collective-permute-start(bf16[512,256]{1,0:T(8,128)(2,1)S(1)} %convolution_convert_fusion.12), channel_id=1, source_target_pairs={{0,8},{8,0},{16,24},{24,16},{1,9},{9,1},{17,25},{25,17},{2,10},{10... | collective-permute-start | bytes 786440 | tf_op jit(solution)/shard_map/ppermute | solution.py:30
  241.2 10.4 %collective-permute-start.35 = (bf16[256,768]{1,0:T(8,128)(2,1)S(1)}, bf16[256,768]{1,0:T(8,128)(2,1)S(1)}, u32[]{:S(2)}, u32[]{:S(2)}) collective-permute-start(bf16[256,768]{1,0:T(8,128)(2,1)S(1)} %add_convert_fusion.3), channel_id=1, source_target_pairs={{0,8},{8,0},{16,24},{24,16},{1,9},{9,1},{17,25},{25,17},{2,10},{10... | collective-permute-start | bytes 1179656 | tf_op jit(solution)/shard_map/ppermute | solution.py:30
  243.8 9.2 %collective-permute-start.36 = (bf16[256,768]{1,0:T(8,128)(2,1)S(1)}, bf16[256,768]{1,0:T(8,128)(2,1)S(1)}, u32[]{:S(2)}, u32[]{:S(2)}) collective-permute-start(bf16[256,768]{1,0:T(8,128)(2,1)S(1)} %add_convert_fusion.2), channel_id=1, source_target_pairs={{0,16},{8,24},{16,0},{24,8},{1,17},{9,25},{17,1},{25,9},{2,18},{10... | collective-permute-start | bytes 1179656 | tf_op jit(solution)/shard_map/ppermute | solution.py:30
  246.6 8.7 %copy-start.31 = (f32[256,768]{1,0:T(8,128)S(1)}, f32[256,768]{1,0:T(8,128)}, u32[]{:S(2)}) copy-start(f32[256,768]{1,0:T(8,128)} %fusion.29) | copy-start | bytes 2359300
  246.6 27.0 %collective-permute-start.32 = (bf16[256,768]{1,0:T(8,128)(2,1)S(1)}, bf16[256,768]{1,0:T(8,128)(2,1)S(1)}, u32[]{:S(2)}, u32[]{:S(2)}) collective-permute-start(bf16[256,768]{1,0:T(8,128)(2,1)S(1)} %add_convert_fusion.1), channel_id=1, source_target_pairs={{0,4},{1,5},{2,6},{3,7},{4,0},{5,1},{6,2},{7,3},{8,12},{9,13},{10,... | collective-permute-start | bytes 1179656 | tf_op jit(solution)/shard_map/ppermute | solution.py:30
  250.1 23.5 %copy-start.4 = (f32[256,768]{1,0:T(8,128)S(1)}, f32[256,768]{1,0:T(8,128)}, u32[]{:S(2)}) copy-start(f32[256,768]{1,0:T(8,128)} %fusion.73) | copy-start | bytes 2359300
  253.1 22.6 %collective-permute-start.38 = (bf16[256,256]{1,0:T(8,128)(2,1)S(1)}, bf16[256,256]{1,0:T(8,128)(2,1)S(1)}, u32[]{:S(2)}, u32[]{:S(2)}) collective-permute-start(bf16[256,256]{1,0:T(8,128)(2,1)S(1)} %add_convert_fusion.20), channel_id=1, source_target_pairs={{0,8},{8,0},{16,24},{24,16},{1,9},{9,1},{17,25},{25,17},{2,10},{10... | collective-permute-start | bytes 393224 | tf_op jit(solution)/shard_map/ppermute | solution.py:30
  253.8 21.9 %collective-permute-start.39 = (bf16[256,256]{1,0:T(8,128)(2,1)S(1)}, bf16[256,256]{1,0:T(8,128)(2,1)S(1)}, u32[]{:S(2)}, u32[]{:S(2)}) collective-permute-start(bf16[256,256]{1,0:T(8,128)(2,1)S(1)} %add_convert_fusion.19), channel_id=1, source_target_pairs={{0,16},{8,24},{16,0},{24,8},{1,17},{9,25},{17,1},{25,9},{2,18},{10... | collective-permute-start | bytes 393224 | tf_op jit(solution)/shard_map/ppermute | solution.py:30
  256.4 22.7 %copy-start.7 = (f32[256,768]{1,0:T(8,128)S(1)}, f32[256,768]{1,0:T(8,128)}, u32[]{:S(2)}) copy-start(f32[256,768]{1,0:T(8,128)} %fusion.74) | copy-start | bytes 2359300
  256.4 22.7 %collective-permute-start.37 = (bf16[256,768]{1,0:T(8,128)(2,1)S(1)}, bf16[256,768]{1,0:T(8,128)(2,1)S(1)}, u32[]{:S(2)}, u32[]{:S(2)}) collective-permute-start(bf16[256,768]{1,0:T(8,128)(2,1)S(1)} %add_convert_fusion), channel_id=1, source_target_pairs={{0,4},{1,5},{2,6},{3,7},{4,0},{5,1},{6,2},{7,3},{8,12},{9,13},{10,... | collective-permute-start | bytes 1179656 | tf_op jit(solution)/shard_map/ppermute | solution.py:30
  275.7 7.3 %collective-permute-start.40 = (bf16[256,256]{1,0:T(8,128)(2,1)S(1)}, bf16[256,256]{1,0:T(8,128)(2,1)S(1)}, u32[]{:S(2)}, u32[]{:S(2)}) collective-permute-start(bf16[256,256]{1,0:T(8,128)(2,1)S(1)} %add_convert_fusion.18), channel_id=1, source_target_pairs={{0,4},{1,5},{2,6},{3,7},{4,0},{5,1},{6,2},{7,3},{8,12},{9,13},{10,... | collective-permute-start | bytes 393224 | tf_op jit(solution)/shard_map/ppermute | solution.py:30
  (38 other events, 68.5 us)
where the time goes:
time: 286 us; the launch traced here: 284 us
  waiting for transfers between devices  71.3 us (25%)
  Pallas kernels  52.3 us (18%)
  starting transfers between devices  48.6 us (17%)
  other arithmetic  41.8 us (15%)
  matrix products  37.1 us (13%)
  local copies, waits for them, and re-layouts  30.7 us (11%)
    ppermute x41, waiting for transfers between devices, swap(): return lax.ppermute(value, axis, [(i, i ^ offset) for i in range(ways)])  71.3 us
    ppermute x41, starting transfers between devices, swap(): return lax.ppermute(value, axis, [(i, i ^ offset) for i in range(ways)])  48.6 us
    dot_general x42, matrix products, partial(): return jnp.dot(left, self.weights[half], preferred_element_type=jnp.float32)  37.1 us
    pallas_call x3, Pallas kernels, pack_columns(): pl.pallas_call(functools.partial(copy_kernel, members=group), grid_spec=p...  21.2 us
    pallas_call x1, Pallas kernels, fill_pages(): pl.pallas_call(pages_kernel, grid_spec=pltpu.PrefetchScalarGridSpec(num_s...  10.4 us
    pallas_call x1, Pallas kernels, token_cells_kernel(): pl.pallas_call(functools.partial(token_kernel, group=group, rows=rows, st...  9.28 us
    unnamed x124, local copies, waits for them, and re-layouts  8.89 us
    convert_element_type x7, other arithmetic, last_far(): far = self.total(1, [0], partial).astype(jnp.bfloat16)  7.96 us
  transfers between devices with their start and end apart: 41, of which 15 were waited for; matrix products, arithmetic and copies ran while one was open for 35% of the time, Pallas kernels for 17%

commit v1 on v0

--- a/solution.py
+++ b/solution.py
@@ -373,12 +373,12 @@
             jobs[turn - levels].last_far()
         if turn + 2 < count:
             jobs[turn + 2].send_weights()
-        elif turn > levels:
-            jobs[turn - levels - 1].close()
         if turn == 0:
             store_last()
         for extra in late.get(turn, ()):
             extra()
+        if turn + 2 >= count and turn > levels:
+            jobs[turn - levels - 1].close()
 
 
 def heads_kernel(near_ref, far_ref, cos_ref, sin_ref, q_ref, kv_ref):
@@ -615,7 +615,7 @@
 
     model_ways_cols = gate_up_weight.shape[1] // 2 // model_ways
     heads_job = Job(order, (heads_here + 2) * HD, heads_done)
-    jobs = [heads_job, *feed_forward_jobs(order, model_ways_cols, heads_job.width)]
+    jobs = [heads_job, *feed_forward_jobs(order, model_ways_cols, 1024)]
     near, far = pack_heads(qkv_weight, head_starts)
     order.done(near)
     heads_job.stored = (near, swap(far, "mp", 1))
@@ -642,7 +642,7 @@
     early = {}
     for i, bit in enumerate(heads_job.bits):
         early.setdefault(min(levels + 2 + i, final), []).append(spread(bit))
-    late = {min(2 * levels + 1, final): [attention, paging]}
+    late = {max(final - 1, *early): [attention, paging]}
     run_jobs(jobs, last_jobs, store_last, early, late)
     hidden = jnp.concatenate([job.result for job in jobs[1:]], axis=1)
     return (held["attended"], hidden, held["kv_cache"])

time: 286 us -> 286 us (level)
  waiting for transfers between devices: 71.3 us -> 114 us
  local copies, waits for them, and re-layouts: 30.7 us -> 16 us
  other arithmetic: 41.8 us -> 29.4 us
  matrix products: 37.1 us -> 31.8 us
  starting transfers between devices: 48.6 us -> 44 us
  Pallas kernels: 52.3 us -> 47.7 us
    ppermute x41 -> x32, waiting for transfers between devices: 71.3 us -> 114 us  [swap(): return lax.ppermute(value, axis, [(i, i ^ offset) for i in range(ways)])]
    dot_general x42 -> x30, matrix products: 37.1 us -> 31.8 us  [partial(): return jnp.dot(left, self.weights[half], preferred_element_type=jnp.float32)]
    pallas_call x3 -> x2, Pallas kernels: 21.2 us -> 16.6 us  [pack_columns(): pl.pallas_call(functools.partial(copy_kernel, members=group), grid_spec=p...]
    ppermute x41 -> x32, starting transfers between devices: 48.6 us -> 44 us  [swap(): return lax.ppermute(value, axis, [(i, i ^ offset) for i in range(ways)])]
    squeeze x13 -> x9, local copies, waits for them, and re-layouts: 6.74 us -> 2.32 us  [send_weights(): self.near, self.far_core = ([near[0]], [far[0]])]
    convert_element_type x14 -> x10, other arithmetic: 7.3 us -> 3.46 us  [leave(): return self.total(half, leaving, partial).astype(jnp.bfloat16)]
    unnamed x124 -> x80, local copies, waits for them, and re-layouts: 8.89 us -> 5.12 us
    squeeze x7 -> x5, local copies, waits for them, and re-layouts: 5.14 us -> 1.86 us  [join_weights(): p[0]]
  transfers between devices with their start and end apart: 41 -> 32, of which waited for: 15 -> 14; matrix products, arithmetic and copies ran while one was open for 35% -> 24% of each run, Pallas kernels for 17% -> 11%
where the time goes in v1:
time: 286 us; the launch traced here: 285 us
  waiting for transfers between devices  114 us (40%)
  Pallas kernels  47.7 us (17%)
  starting transfers between devices  44 us (15%)
  matrix products  31.8 us (11%)
  other arithmetic  29.4 us (10%)
  local copies, waits for them, and re-layouts  16 us (6%)
    ppermute x32, waiting for transfers between devices, swap(): return lax.ppermute(value, axis, [(i, i ^ offset) for i in range(ways)])  114 us
    ppermute x32, starting transfers between devices, swap(): return lax.ppermute(value, axis, [(i, i ^ offset) for i in range(ways)])  44 us
    dot_general x30, matrix products, partial(): return jnp.dot(left, self.weights[half], preferred_element_type=jnp.float32)  31.8 us
    pallas_call x2, Pallas kernels, pack_columns(): pl.pallas_call(functools.partial(copy_kernel, members=group), grid_spec=p...  16.6 us
    pallas_call x1, Pallas kernels, fill_pages(): pl.pallas_call(pages_kernel, grid_spec=pltpu.PrefetchScalarGridSpec(num_s...  10.2 us
    pallas_call x1, Pallas kernels, token_cells_kernel(): pl.pallas_call(functools.partial(token_kernel, group=group, rows=rows, st...  9.3 us
    add x4, other arithmetic, finish(): both = near + far.astype(jnp.float32)  6.04 us
    convert_element_type x5, other arithmetic, last_far(): far = self.total(1, [0], partial).astype(jnp.bfloat16)  5.73 us
  transfers between devices with their start and end apart: 32, of which 14 were waited for; matrix products, arithmetic and copies ran while one was open for 24% of the time, Pallas kernels for 11%

profile of v1, /device:TPU:0, one launch (start us, length us, event | category | flops | bytes accessed | tf_op | source)
XLA Modules:
  0.0 284.7 jit_solution(18022749715038876534)
XLA Ops:
  0.6 3.6 %pack_heads.1 = (bf16[2,160,1536]{2,1,0:T(8,128)(2,1)}, bf16[2,160,1536]{2,1,0:T(8,128)(2,1)}) custom-call(s32[1]{0:T(128)} %bitcast.3.at_ref, f32[160,6144]{1,0:T(8,128)} %refs_11_.1, f32[160,6144]{1,0:T(8,128)} %refs_11_.1, f32[160,6144]{1,0:T(8,128)} %refs_11_.1, f32[160,6144]{1,0:T(8,128)} %refs_11_.1, f32[160,6144]{1,0:T(8,128)} %refs_11_.1, ...), custom_call_target="tpu_custom_call" | custom-call | flops 1 | bytes 1 | tf_op jit(solution)/shard_map/pack_heads/pallas_call | solution.py:192
  4.2 4.6 %pack_columns.2 = (bf16[2,160,2048]{2,1,0:T(8,128)(2,1)}, bf16[2,160,2048]{2,1,0:T(8,128)(2,1)}) custom-call(s32[1]{0:T(128)} %bitcast.3.at_ref, f32[160,32768]{1,0:T(8,128)} %refs_3_.3, f32[160,32768]{1,0:T(8,128)} %refs_3_.3, f32[160,32768]{1,0:T(8,128)} %refs_3_.3, f32[160,32768]{1,0:T(8,128)} %refs_3_.3), custom_call_target="tpu_custom_call" | custom-call | flops 1 | bytes 1 | tf_op jit(solution)/shard_map/pack_columns/pallas_call | solution.py:154
  9.4 9.3 %token_cells.1 = (bf16[256,640]{1,0:T(8,128)(2,1)}, bf16[256,640]{1,0:T(8,128)(2,1)}, bf16[2,256,640]{2,1,0:T(8,128)(2,1)}, bf16[2,256,640]{2,1,0:T(8,128)(2,1)}, bf16[2,256,640]{2,1,0:T(8,128)(2,1)}) custom-call(s32[3]{0:T(128)} %pad_add_fusion.at_ref, bf16[256,5120]{1,0:T(8,128)(2,1)} %refs_0_.3, bf16[256,5120]{1,0:T(8,128)(2,1)} %refs_1_.3, ...), custom_call_target="tpu_custom_call" | custom-call | flops 1 | bytes 1 | tf_op jit(solution)/shard_map/token_cells/pallas_call | solution.py:99
  18.7 3.0 %collective-permute-start.3 = (bf16[2,256,640]{2,1,0:T(8,128)(2,1)}, bf16[2,256,640]{2,1,0:T(8,128)(2,1)}, u32[]{:S(2)}, u32[]{:S(2)}) collective-permute-start(bf16[2,256,640]{2,1,0:T(8,128)(2,1)} %get-tuple-element.111), channel_id=1, source_target_pairs={{0,8},{8,0},{16,24},{24,16},{1,9},{9,1},{17,25},{25,17},{2,10},{10... | collective-permute-start | bytes 1966088 | tf_op jit(solution)/shard_map/ppermute | solution.py:30
  21.6 1.5 collective-permute-start.4
  29.4 2.1 collective-permute-start.1
  32.3 1.4 slice_bitcast_fusion.13
  33.8 1.2 pad_maximum_fusion.6
  35.0 12.0 %pack_columns.3 = (bf16[2,160,6144]{2,1,0:T(8,128)(2,1)}, bf16[2,160,6144]{2,1,0:T(8,128)(2,1)}) custom-call(s32[1]{0:T(128)} %bitcast.3.at_ref, f32[160,32768]{1,0:T(8,128)} %refs_3_.3, f32[160,32768]{1,0:T(8,128)} %refs_3_.3, f32[160,32768]{1,0:T(8,128)} %refs_3_.3, f32[160,32768]{1,0:T(8,128)} %refs_3_.3), custom_call_target="tpu_custom_call" | custom-call | flops 1 | bytes 1 | tf_op jit(solution)/shard_map/pack_columns/pallas_call | solution.py:154
  47.2 6.4 %collective-permute-done.1 = bf16[2,160,1536]{2,1,0:T(8,128)(2,1)S(1)} collective-permute-done((bf16[2,160,1536]{2,1,0:T(8,128)(2,1)}, bf16[2,160,1536]{2,1,0:T(8,128)(2,1)S(1)}, u32[]{:S(2)}, u32[]{:S(2)}) %collective-permute-start.1) | collective-permute-done | bytes 983072 | tf_op jit(solution)/shard_map/ppermute | solution.py:30
  53.6 1.7 collective-permute-start.8
  57.6 1.4 slice_bitcast_fusion.20
  59.0 1.6 fusion.12
  63.7 1.6 collective-permute-start.6
  65.3 1.5 collective-permute-start.7
  67.7 17.6 %collective-permute-done.8 = bf16[2,160,2048]{2,1,0:T(8,128)(2,1)S(1)} collective-permute-done((bf16[2,160,2048]{2,1,0:T(8,128)(2,1)S(1)}, bf16[2,160,2048]{2,1,0:T(8,128)(2,1)S(1)}, u32[]{:S(2)}, u32[]{:S(2)}) %collective-permute-start.8) | collective-permute-done | bytes 1310752 | tf_op jit(solution)/shard_map/ppermute | solution.py:30
  87.7 1.7 collective-permute-start.10
  89.4 1.5 collective-permute-start.11
  94.0 1.5 fusion.20
  96.7 15.1 %collective-permute-done.14 = bf16[2,160,2048]{2,1,0:T(8,128)(2,1)S(1)} collective-permute-done((bf16[2,160,2048]{2,1,0:T(8,128)(2,1)S(1)}, bf16[2,160,2048]{2,1,0:T(8,128)(2,1)S(1)}, u32[]{:S(2)}, u32[]{:S(2)}) %collective-permute-start.14) | collective-permute-done | bytes 1310752 | tf_op jit(solution)/shard_map/ppermute | solution.py:30
  111.8 1.4 collective-permute-start.18
  115.6 3.4 %collective-permute-done.12 = bf16[256,768]{1,0:T(8,128)(2,1)S(1)} collective-permute-done((bf16[256,768]{1,0:T(8,128)(2,1)S(1)}, bf16[256,768]{1,0:T(8,128)(2,1)S(1)}, u32[]{:S(2)}, u32[]{:S(2)}) %collective-permute-start.12) | collective-permute-done | bytes 393248 | tf_op jit(solution)/shard_map/ppermute | solution.py:30
  121.2 1.3 collective-permute-start.17
  122.7 2.6 collective-permute-start.15
  126.8 2.0 collective-permute-start.19
  128.8 1.6 fusion.24
  130.4 1.6 fusion.19
  131.9 20.1 %collective-permute-done.18 = bf16[2,160,2048]{2,1,0:T(8,128)(2,1)S(1)} collective-permute-done((bf16[2,160,2048]{2,1,0:T(8,128)(2,1)S(1)}, bf16[2,160,2048]{2,1,0:T(8,128)(2,1)S(1)}, u32[]{:S(2)}, u32[]{:S(2)}) %collective-permute-start.18) | collective-permute-done | bytes 1310752 | tf_op jit(solution)/shard_map/ppermute | solution.py:30
  153.4 2.5 fusion.18
  156.0 1.6 fusion.23
  160.9 1.6 fusion.14
  162.5 1.6 fusion.48
  164.9 1.5 pad_maximum_fusion.2
  166.4 1.4 collective-permute-start.22
  167.9 1.3 pad_maximum_fusion.3
  169.2 1.5 collective-permute-start.23
  171.7 1.7 collective-permute-start.21
  174.4 2.3 finish_heads.1
  176.7 9.5 %collective-permute-done.19 = bf16[2,160,2048]{2,1,0:T(8,128)(2,1)} collective-permute-done((bf16[2,160,2048]{2,1,0:T(8,128)(2,1)}, bf16[2,160,2048]{2,1,0:T(8,128)(2,1)}, u32[]{:S(2)}, u32[]{:S(2)}) %collective-permute-start.19) | collective-permute-done | bytes 1310752 | tf_op jit(solution)/shard_map/ppermute | solution.py:30
  186.2 1.4 slice_bitcast_fusion.2
  188.7 2.0 collective-permute-start.20
  193.3 1.6 fusion.50
  194.9 3.7 %collective-permute-done.22 = bf16[768,1024]{1,0:T(8,128)(2,1)} collective-permute-done((bf16[768,1024]{1,0:T(8,128)(2,1)}, bf16[768,1024]{1,0:T(8,128)(2,1)}, u32[]{:S(2)}, u32[]{:S(2)}) %collective-permute-start.22) | collective-permute-done | bytes 1572896 | tf_op jit(solution)/shard_map/ppermute | solution.py:30
  198.6 3.7 %collective-permute-done.23 = bf16[768,1024]{1,0:T(8,128)(2,1)} collective-permute-done((bf16[768,1024]{1,0:T(8,128)(2,1)}, bf16[768,1024]{1,0:T(8,128)(2,1)}, u32[]{:S(2)}, u32[]{:S(2)}) %collective-permute-start.23) | collective-permute-done | bytes 1572896 | tf_op jit(solution)/shard_map/ppermute | solution.py:30
  203.6 1.4 collective-permute-start.26
  206.3 1.9 collective-permute-start.27
  208.2 1.6 fusion.17
  211.5 1.4 add_convert_fusion.4
  212.9 1.7 collective-permute-start.25
  214.6 1.4 convert_add_fusion.3
  217.3 18.6 %collective-permute-done.26 = bf16[768,1024]{1,0:T(8,128)(2,1)S(1)} collective-permute-done((bf16[768,1024]{1,0:T(8,128)(2,1)S(1)}, bf16[768,1024]{1,0:T(8,128)(2,1)S(1)}, u32[]{:S(2)}, u32[]{:S(2)}) %collective-permute-start.26) | collective-permute-done | bytes 1572896 | tf_op jit(solution)/shard_map/ppermute | solution.py:30
  235.9 4.8 %collective-permute-done.27 = bf16[768,1024]{1,0:T(8,128)(2,1)S(1)} collective-permute-done((bf16[768,1024]{1,0:T(8,128)(2,1)S(1)}, bf16[768,1024]{1,0:T(8,128)(2,1)S(1)}, u32[]{:S(2)}, u32[]{:S(2)}) %collective-permute-start.27) | collective-permute-done | bytes 1572896 | tf_op jit(solution)/shard_map/ppermute | solution.py:30
  240.9 1.9 collective-permute-start.28
  243.3 2.1 add_convert_fusion.1
  245.4 2.4 collective-permute-start.30
  247.9 1.5 convert_add_fusion.2
  250.1 2.1 collective-permute-done.29
  253.3 1.7 collective-permute-start.31
  255.7 5.7 %attend.1 = bf16[256,512]{1,0:T(8,128)(2,1)} custom-call(s32[1]{0:T(128)} %bitcast.at_ref, bf16[256,512]{1,0:T(8,128)(2,1)} %get-tuple-element.154.q_ref, s32[256,1]{1,0:T(8,128)} %copy.14.first_ref, s32[256,1]{1,0:T(8,128)} %iota_add_fusion.token_ref, bf16[256,256]{1,0:T(8,128)(2,1)} %get-tuple-element.181.refs_0_, bf16[256,256]{1,0:T(8,128)(2,1)} %copy-done.14, ...), custom_call_target="tpu_custom_call" | custom-call | flops 1 | bytes 1 | tf_op jit(solution)/shard_map/attend/pallas_call | solution.py:457
  261.4 10.2 %fill_pages.1 = bf16[96,128,256]{2,1,0:T(8,128)(2,1)} custom-call(s32[1]{0:T(128)} %bitcast.at_ref, s32[96]{0:T(128)} %get-tuple-element.191.start_ref, s32[96]{0:T(128)} %get-tuple-element.192.count_ref, bf16[256,256]{1,0:T(8,128)(2,1)} %get-tuple-element.181.refs_0_, bf16[256,256]{1,0:T(8,128)(2,1)} %copy-done.14, bf16[512,256]{1,0:T(8,128)(2,1)} %copy-done.15), custom_call_target="tpu_custom_call" | custom-call | flops 1 | bytes 1 | tf_op jit(solution)/shard_map/fill_pages/pallas_call | solution.py:504
  271.7 4.5 %collective-permute-done.30 = bf16[256,1024]{1,0:T(8,128)(2,1)} collective-permute-done((bf16[256,1024]{1,0:T(8,128)(2,1)}, bf16[256,1024]{1,0:T(8,128)(2,1)}, u32[]{:S(2)}, u32[]{:S(2)}) %collective-permute-start.30) | collective-permute-done | bytes 524320 | tf_op jit(solution)/shard_map/ppermute | solution.py:30
  276.2 1.6 convert_add_fusion.1
  278.0 3.9 %collective-permute-done.31 = bf16[256,1024]{1,0:T(8,128)(2,1)} collective-permute-done((bf16[256,1024]{1,0:T(8,128)(2,1)}, bf16[256,1024]{1,0:T(8,128)(2,1)}, u32[]{:S(2)}, u32[]{:S(2)}) %collective-permute-start.31) | collective-permute-done | bytes 524320 | tf_op jit(solution)/shard_map/ppermute | solution.py:30
  281.9 1.5 convert_add_fusion
  (215 shorter events, 47.9 us)
Async XLA Ops:
  9.4 15.0 %copy-start.37 = (s32[6]{0:T(128)S(1)}, s32[6]{0:T(128)}, u32[]{:S(2)}) copy-start(s32[6]{0:T(128)} %param.15) | copy-start | bytes 76
  9.4 16.1 %copy-start.36 = (s32[64,4]{0,1:T(4,128)S(1)}, s32[64,4]{0,1:T(4,128)}, u32[]{:S(2)}) copy-start(s32[64,4]{0,1:T(4,128)} %param.17) | copy-start | bytes 3076
  9.4 16.5 %copy-start.38 = (s32[64]{0:T(128)S(1)}, s32[64]{0:T(128)}, u32[]{:S(2)}) copy-start(s32[64]{0:T(128)} %param.16) | copy-start | bytes 772
  18.7 9.6 %copy-start.22 = (bf16[2,160,1536]{2,1,0:T(8,128)(2,1)S(1)}, bf16[2,160,1536]{2,1,0:T(8,128)(2,1)}, u32[]{:S(2)}) copy-start(bf16[2,160,1536]{2,1,0:T(8,128)(2,1)} %get-tuple-element.103) | copy-start | bytes 2949124
  18.7 37.7 %collective-permute-start.3 = (bf16[2,256,640]{2,1,0:T(8,128)(2,1)}, bf16[2,256,640]{2,1,0:T(8,128)(2,1)}, u32[]{:S(2)}, u32[]{:S(2)}) collective-permute-start(bf16[2,256,640]{2,1,0:T(8,128)(2,1)} %get-tuple-element.111), channel_id=1, source_target_pairs={{0,8},{8,0},{16,24},{24,16},{1,9},{9,1},{17,25},{25,17},{2,10},{10... | collective-permute-start | bytes 1966088 | tf_op jit(solution)/shard_map/ppermute | solution.py:30
  21.6 34.7 %collective-permute-start.4 = (bf16[2,256,640]{2,1,0:T(8,128)(2,1)}, bf16[2,256,640]{2,1,0:T(8,128)(2,1)S(1)}, u32[]{:S(2)}, u32[]{:S(2)}) collective-permute-start(bf16[2,256,640]{2,1,0:T(8,128)(2,1)} %get-tuple-element.112), channel_id=1, source_target_pairs={{0,16},{8,24},{16,0},{24,8},{1,17},{9,25},{17,1},{25,9},{2,18},{10... | collective-permute-start | bytes 1966088 | tf_op jit(solution)/shard_map/ppermute | solution.py:30
  23.2 33.2 %collective-permute-start.5 = (bf16[2,256,640]{2,1,0:T(8,128)(2,1)}, bf16[2,256,640]{2,1,0:T(8,128)(2,1)}, u32[]{:S(2)}, u32[]{:S(2)}) collective-permute-start(bf16[2,256,640]{2,1,0:T(8,128)(2,1)} %get-tuple-element.113), channel_id=1, source_target_pairs={{0,24},{8,16},{16,8},{24,0},{1,25},{9,17},{17,9},{25,1},{2,26},{10... | collective-permute-start | bytes 1966088 | tf_op jit(solution)/shard_map/ppermute | solution.py:30
  23.2 5.1 %collective-permute-start = (bf16[2,160,1536]{2,1,0:T(8,128)(2,1)}, bf16[2,160,1536]{2,1,0:T(8,128)(2,1)S(1)}, u32[]{:S(2)}, u32[]{:S(2)}) collective-permute-start(bf16[2,160,1536]{2,1,0:T(8,128)(2,1)} %get-tuple-element.102), channel_id=1, source_target_pairs={{0,1},{1,0},{2,3},{3,2},{4,5},{5,4},{6,7},{7,6},{8,9},{9,8},{10,11... | collective-permute-start | bytes 2949128 | tf_op jit(solution)/shard_map/ppermute | solution.py:30
  23.2 9.1 %collective-permute-start.2 = (bf16[2,160,2048]{2,1,0:T(8,128)(2,1)}, bf16[2,160,2048]{2,1,0:T(8,128)(2,1)}, u32[]{:S(2)}, u32[]{:S(2)}) collective-permute-start(bf16[2,160,2048]{2,1,0:T(8,128)(2,1)} %get-tuple-element.105), channel_id=1, source_target_pairs={{0,1},{1,0},{2,3},{3,2},{4,5},{5,4},{6,7},{7,6},{8,9},{9,8},{10,11... | collective-permute-start | bytes 3932168 | tf_op jit(solution)/shard_map/ppermute | solution.py:30
  29.4 24.2 %collective-permute-start.1 = (bf16[2,160,1536]{2,1,0:T(8,128)(2,1)}, bf16[2,160,1536]{2,1,0:T(8,128)(2,1)S(1)}, u32[]{:S(2)}, u32[]{:S(2)}) collective-permute-start(bf16[2,160,1536]{2,1,0:T(8,128)(2,1)} %pad_maximum_fusion.19), channel_id=1, source_target_pairs={{0,2},{1,3},{2,0},{3,1},{4,6},{5,7},{6,4},{7,5},{8,10},{9,11},{10,... | collective-permute-start | bytes 2949128 | tf_op jit(solution)/shard_map/ppermute | solution.py:30
  31.5 2.2 copy-start.11
  47.0 19.8 %collective-permute-start.9 = (bf16[2,160,6144]{2,1,0:T(8,128)(2,1)}, bf16[2,160,6144]{2,1,0:T(8,128)(2,1)S(1)}, u32[]{:S(2)}, u32[]{:S(2)}) collective-permute-start(bf16[2,160,6144]{2,1,0:T(8,128)(2,1)} %get-tuple-element.119), channel_id=1, source_target_pairs={{0,1},{1,0},{2,3},{3,2},{4,5},{5,4},{6,7},{7,6},{8,9},{9,8},{10,11... | collective-permute-start | bytes 11796488 | tf_op jit(solution)/shard_map/ppermute | solution.py:30
  47.0 6.6 %copy-start.12 = (bf16[2,160,2048]{2,1,0:T(8,128)(2,1)S(1)}, bf16[2,160,2048]{2,1,0:T(8,128)(2,1)}, u32[]{:S(2)}) copy-start(bf16[2,160,2048]{2,1,0:T(8,128)(2,1)} %pad_maximum_fusion.6) | copy-start | bytes 3932164
  53.6 31.7 %collective-permute-start.8 = (bf16[2,160,2048]{2,1,0:T(8,128)(2,1)S(1)}, bf16[2,160,2048]{2,1,0:T(8,128)(2,1)S(1)}, u32[]{:S(2)}, u32[]{:S(2)}) collective-permute-start(bf16[2,160,2048]{2,1,0:T(8,128)(2,1)S(1)} %copy-done.12), channel_id=1, source_target_pairs={{0,2},{1,3},{2,0},{3,1},{4,6},{5,7},{6,4},{7,5},{8,10},{9,11},{10,... | collective-permute-start | bytes 3932168 | tf_op jit(solution)/shard_map/ppermute | solution.py:30
  57.5 101.8 %copy-start.26 = (bf16[256,640]{1,0:T(8,128)(2,1)}, bf16[256,640]{1,0:T(8,128)(2,1)S(1)}, u32[]{:S(2)}) copy-start(bf16[256,640]{1,0:T(8,128)(2,1)S(1)} %get-tuple-element.259) | copy-start | bytes 983044
  57.5 1.5 copy-start.35
  57.6 94.6 %copy-start.28 = (bf16[256,640]{1,0:T(8,128)(2,1)}, bf16[256,640]{1,0:T(8,128)(2,1)S(1)}, u32[]{:S(2)}) copy-start(bf16[256,640]{1,0:T(8,128)(2,1)S(1)} %get-tuple-element.257) | copy-start | bytes 983044
  59.0 100.3 %copy-start.30 = (bf16[256,640]{1,0:T(8,128)(2,1)}, bf16[256,640]{1,0:T(8,128)(2,1)S(1)}, u32[]{:S(2)}) copy-start(bf16[256,640]{1,0:T(8,128)(2,1)S(1)} %get-tuple-element.247) | copy-start | bytes 983044
  59.0 1.6 copy-start.34
  62.9 4.0 %copy-start.4 = (bf16[2,160,6144]{2,1,0:T(8,128)(2,1)S(1)}, bf16[2,160,6144]{2,1,0:T(8,128)(2,1)}, u32[]{:S(2)}) copy-start(bf16[2,160,6144]{2,1,0:T(8,128)(2,1)} %get-tuple-element.141) | copy-start | bytes 11796484
  63.7 23.9 %collective-permute-start.6 = (bf16[512,768]{1,0:T(8,128)(2,1)S(1)}, bf16[512,768]{1,0:T(8,128)(2,1)S(1)}, u32[]{:S(2)}, u32[]{:S(2)}) collective-permute-start(bf16[512,768]{1,0:T(8,128)(2,1)S(1)} %convolution_convert_fusion.9), channel_id=1, source_target_pairs={{0,16},{8,24},{16,0},{24,8},{1,17},{9,25},{17,1},{25,9},{2,18},{10... | collective-permute-start | bytes 2359304 | tf_op jit(solution)/shard_map/ppermute | solution.py:30
  65.3 22.4 %collective-permute-start.7 = (bf16[512,768]{1,0:T(8,128)(2,1)S(1)}, bf16[512,768]{1,0:T(8,128)(2,1)S(1)}, u32[]{:S(2)}, u32[]{:S(2)}) collective-permute-start(bf16[512,768]{1,0:T(8,128)(2,1)S(1)} %convolution_convert_fusion.8), channel_id=1, source_target_pairs={{0,8},{8,0},{16,24},{24,16},{1,9},{9,1},{17,25},{25,17},{2,10},{10... | collective-permute-start | bytes 2359304 | tf_op jit(solution)/shard_map/ppermute | solution.py:30
  67.2 44.7 %collective-permute-start.14 = (bf16[2,160,2048]{2,1,0:T(8,128)(2,1)S(1)}, bf16[2,160,2048]{2,1,0:T(8,128)(2,1)S(1)}, u32[]{:S(2)}, u32[]{:S(2)}) collective-permute-start(bf16[2,160,2048]{2,1,0:T(8,128)(2,1)S(1)} %pad_maximum_fusion.7), channel_id=1, source_target_pairs={{0,2},{1,3},{2,0},{3,1},{4,6},{5,7},{6,4},{7,5},{8,10},{9,11},{10,... | collective-permute-start | bytes 3932168 | tf_op jit(solution)/shard_map/ppermute | solution.py:30
  87.7 31.3 %collective-permute-start.10 = (bf16[512,1024]{1,0:T(8,128)(2,1)S(1)}, bf16[512,1024]{1,0:T(8,128)(2,1)S(1)}, u32[]{:S(2)}, u32[]{:S(2)}) collective-permute-start(bf16[512,1024]{1,0:T(8,128)(2,1)S(1)} %convolution_convert_fusion.7), channel_id=1, source_target_pairs={{0,16},{8,24},{16,0},{24,8},{1,17},{9,25},{17,1},{25,9},{2,18},{10... | collective-permute-start | bytes 3145736 | tf_op jit(solution)/shard_map/ppermute | solution.py:30
  89.4 29.6 %collective-permute-start.11 = (bf16[512,1024]{1,0:T(8,128)(2,1)S(1)}, bf16[512,1024]{1,0:T(8,128)(2,1)S(1)}, u32[]{:S(2)}, u32[]{:S(2)}) collective-permute-start(bf16[512,1024]{1,0:T(8,128)(2,1)S(1)} %convolution_convert_fusion.6), channel_id=1, source_target_pairs={{0,8},{8,0},{16,24},{24,16},{1,9},{9,1},{17,25},{25,17},{2,10},{10... | collective-permute-start | bytes 3145736 | tf_op jit(solution)/shard_map/ppermute | solution.py:30
  91.0 28.0 %collective-permute-start.12 = (bf16[256,768]{1,0:T(8,128)(2,1)S(1)}, bf16[256,768]{1,0:T(8,128)(2,1)S(1)}, u32[]{:S(2)}, u32[]{:S(2)}) collective-permute-start(bf16[256,768]{1,0:T(8,128)(2,1)S(1)} %add_convert_fusion.14), channel_id=1, source_target_pairs={{0,8},{8,0},{16,24},{24,16},{1,9},{9,1},{17,25},{25,17},{2,10},{10... | collective-permute-start | bytes 1179656 | tf_op jit(solution)/shard_map/ppermute | solution.py:30
  91.6 27.3 %collective-permute-start.13 = (bf16[256,768]{1,0:T(8,128)(2,1)S(1)}, bf16[256,768]{1,0:T(8,128)(2,1)S(1)}, u32[]{:S(2)}, u32[]{:S(2)}) collective-permute-start(bf16[256,768]{1,0:T(8,128)(2,1)S(1)} %add_convert_fusion.13), channel_id=1, source_target_pairs={{0,16},{8,24},{16,0},{24,8},{1,17},{9,25},{17,1},{25,9},{2,18},{10... | collective-permute-start | bytes 1179656 | tf_op jit(solution)/shard_map/ppermute | solution.py:30
  111.8 40.1 %collective-permute-start.18 = (bf16[2,160,2048]{2,1,0:T(8,128)(2,1)S(1)}, bf16[2,160,2048]{2,1,0:T(8,128)(2,1)S(1)}, u32[]{:S(2)}, u32[]{:S(2)}) collective-permute-start(bf16[2,160,2048]{2,1,0:T(8,128)(2,1)S(1)} %pad_maximum_fusion.10), channel_id=1, source_target_pairs={{0,2},{1,3},{2,0},{3,1},{4,6},{5,7},{6,4},{7,5},{8,10},{9,11},{10,... | collective-permute-start | bytes 3932168 | tf_op jit(solution)/shard_map/ppermute | solution.py:30
  120.0 44.7 %collective-permute-start.16 = (bf16[768,1024]{1,0:T(8,128)(2,1)S(1)}, bf16[768,1024]{1,0:T(8,128)(2,1)S(1)}, u32[]{:S(2)}, u32[]{:S(2)}) collective-permute-start(bf16[768,1024]{1,0:T(8,128)(2,1)S(1)} %pad_maximum_fusion), channel_id=1, source_target_pairs={{0,16},{8,24},{16,0},{24,8},{1,17},{9,25},{17,1},{25,9},{2,18},{10... | collective-permute-start | bytes 4718600 | tf_op jit(solution)/shard_map/ppermute | solution.py:30
  121.2 43.5 %collective-permute-start.17 = (bf16[768,1024]{1,0:T(8,128)(2,1)S(1)}, bf16[768,1024]{1,0:T(8,128)(2,1)S(1)}, u32[]{:S(2)}, u32[]{:S(2)}) collective-permute-start(bf16[768,1024]{1,0:T(8,128)(2,1)S(1)} %pad_maximum_fusion.1), channel_id=1, source_target_pairs={{0,8},{8,0},{16,24},{24,16},{1,9},{9,1},{17,25},{25,17},{2,10},{10... | collective-permute-start | bytes 4718600 | tf_op jit(solution)/shard_map/ppermute | solution.py:30
  122.7 50.7 %collective-permute-start.15 = (bf16[256,768]{1,0:T(8,128)(2,1)S(1)}, bf16[256,768]{1,0:T(8,128)(2,1)S(1)}, u32[]{:S(2)}, u32[]{:S(2)}) collective-permute-start(bf16[256,768]{1,0:T(8,128)(2,1)S(1)} %add_convert_fusion.12), channel_id=1, source_target_pairs={{0,4},{1,5},{2,6},{3,7},{4,0},{5,1},{6,2},{7,3},{8,12},{9,13},{10,... | collective-permute-start | bytes 1179656 | tf_op jit(solution)/shard_map/ppermute | solution.py:30
  126.8 59.4 %collective-permute-start.19 = (bf16[2,160,2048]{2,1,0:T(8,128)(2,1)}, bf16[2,160,2048]{2,1,0:T(8,128)(2,1)}, u32[]{:S(2)}, u32[]{:S(2)}) collective-permute-start(bf16[2,160,2048]{2,1,0:T(8,128)(2,1)} %pad_maximum_fusion.13), channel_id=1, source_target_pairs={{0,2},{1,3},{2,0},{3,1},{4,6},{5,7},{6,4},{7,5},{8,10},{9,11},{10,... | collective-permute-start | bytes 3932168 | tf_op jit(solution)/shard_map/ppermute | solution.py:30
  164.7 3.1 %copy-start.6 = (bf16[768,1024]{1,0:T(8,128)(2,1)}, bf16[768,1024]{1,0:T(8,128)(2,1)S(1)}, u32[]{:S(2)}) copy-start(bf16[768,1024]{1,0:T(8,128)(2,1)S(1)} %collective-permute-done.16) | copy-start | bytes 4718596
  164.7 6.0 %copy-start.5 = (bf16[768,1024]{1,0:T(8,128)(2,1)}, bf16[768,1024]{1,0:T(8,128)(2,1)S(1)}, u32[]{:S(2)}) copy-start(bf16[768,1024]{1,0:T(8,128)(2,1)S(1)} %collective-permute-done.17) | copy-start | bytes 4718596
  166.4 32.2 %collective-permute-start.22 = (bf16[768,1024]{1,0:T(8,128)(2,1)}, bf16[768,1024]{1,0:T(8,128)(2,1)}, u32[]{:S(2)}, u32[]{:S(2)}) collective-permute-start(bf16[768,1024]{1,0:T(8,128)(2,1)} %pad_maximum_fusion.2), channel_id=1, source_target_pairs={{0,16},{8,24},{16,0},{24,8},{1,17},{9,25},{17,1},{25,9},{2,18},{10... | collective-permute-start | bytes 4718600 | tf_op jit(solution)/shard_map/ppermute | solution.py:30
  169.2 33.1 %collective-permute-start.23 = (bf16[768,1024]{1,0:T(8,128)(2,1)}, bf16[768,1024]{1,0:T(8,128)(2,1)}, u32[]{:S(2)}, u32[]{:S(2)}) collective-permute-start(bf16[768,1024]{1,0:T(8,128)(2,1)} %pad_maximum_fusion.3), channel_id=1, source_target_pairs={{0,8},{8,0},{16,24},{24,16},{1,9},{9,1},{17,25},{25,17},{2,10},{10... | collective-permute-start | bytes 4718600 | tf_op jit(solution)/shard_map/ppermute | solution.py:30
  171.7 42.9 %collective-permute-start.21 = (bf16[256,1024]{1,0:T(8,128)(2,1)}, bf16[256,1024]{1,0:T(8,128)(2,1)}, u32[]{:S(2)}, u32[]{:S(2)}) collective-permute-start(bf16[256,1024]{1,0:T(8,128)(2,1)} %add_convert_fusion.7), channel_id=1, source_target_pairs={{0,4},{1,5},{2,6},{3,7},{4,0},{5,1},{6,2},{7,3},{8,12},{9,13},{10,... | collective-permute-start | bytes 1572872 | tf_op jit(solution)/shard_map/ppermute | solution.py:30
  173.4 1.0 copy-start.25
  187.7 3.0 %copy-start.27 = (bf16[256,640]{1,0:T(8,128)(2,1)S(1)}, bf16[256,640]{1,0:T(8,128)(2,1)}, u32[]{:S(2)}) copy-start(bf16[256,640]{1,0:T(8,128)(2,1)} %copy-done.26) | copy-start | bytes 983044
  187.7 3.0 %copy-start.29 = (bf16[256,640]{1,0:T(8,128)(2,1)S(1)}, bf16[256,640]{1,0:T(8,128)(2,1)}, u32[]{:S(2)}) copy-start(bf16[256,640]{1,0:T(8,128)(2,1)} %copy-done.28) | copy-start | bytes 983044
  187.7 3.0 %copy-start.32 = (bf16[160,1024]{1,0:T(8,128)(2,1)S(1)}, bf16[160,1024]{1,0:T(8,128)(2,1)}, u32[]{:S(2)}) copy-start(bf16[160,1024]{1,0:T(8,128)(2,1)} %get-tuple-element.227) | copy-start | bytes 983044
  187.8 2.9 %copy-start.33 = (bf16[160,1024]{1,0:T(8,128)(2,1)S(1)}, bf16[160,1024]{1,0:T(8,128)(2,1)}, u32[]{:S(2)}) copy-start(bf16[160,1024]{1,0:T(8,128)(2,1)} %get-tuple-element.223) | copy-start | bytes 983044
  188.7 27.5 %collective-permute-start.20 = (bf16[256,256]{1,0:T(8,128)(2,1)S(1)}, bf16[256,256]{1,0:T(8,128)(2,1)S(1)}, u32[]{:S(2)}, u32[]{:S(2)}) collective-permute-start(bf16[256,256]{1,0:T(8,128)(2,1)S(1)} %copy-done.13), channel_id=1, source_target_pairs={{0,8},{8,0},{16,24},{24,16},{1,9},{9,1},{17,25},{25,17},{2,10},{10... | collective-permute-start | bytes 393224 | tf_op jit(solution)/shard_map/ppermute | solution.py:30
  193.3 9.0 %copy-start.3 = (f32[256,1024]{1,0:T(8,128)S(1)}, f32[256,1024]{1,0:T(8,128)}, u32[]{:S(2)}) copy-start(f32[256,1024]{1,0:T(8,128)} %fusion.14) | copy-start | bytes 3145732
  203.5 1.5 copy-start.20
  203.6 32.3 %collective-permute-start.26 = (bf16[768,1024]{1,0:T(8,128)(2,1)S(1)}, bf16[768,1024]{1,0:T(8,128)(2,1)S(1)}, u32[]{:S(2)}, u32[]{:S(2)}) collective-permute-start(bf16[768,1024]{1,0:T(8,128)(2,1)S(1)} %pad_maximum_fusion.4), channel_id=1, source_target_pairs={{0,16},{8,24},{16,0},{24,8},{1,17},{9,25},{17,1},{25,9},{2,18},{10... | collective-permute-start | bytes 4718600 | tf_op jit(solution)/shard_map/ppermute | solution.py:30
  206.3 34.4 %collective-permute-start.27 = (bf16[768,1024]{1,0:T(8,128)(2,1)S(1)}, bf16[768,1024]{1,0:T(8,128)(2,1)S(1)}, u32[]{:S(2)}, u32[]{:S(2)}) collective-permute-start(bf16[768,1024]{1,0:T(8,128)(2,1)S(1)} %pad_maximum_fusion.5), channel_id=1, source_target_pairs={{0,8},{8,0},{16,24},{24,16},{1,9},{9,1},{17,25},{25,17},{2,10},{10... | collective-permute-start | bytes 4718600 | tf_op jit(solution)/shard_map/ppermute | solution.py:30
  209.8 1.4 copy-start.7
  209.8 1.7 copy-start.19
  211.5 3.1 %copy-start.17 = (bf16[512,1024]{1,0:T(8,128)(2,1)S(1)}, bf16[512,1024]{1,0:T(8,128)(2,1)}, u32[]{:S(2)}) copy-start(bf16[512,1024]{1,0:T(8,128)(2,1)} %copy-done.16) | copy-start | bytes 3145732
  212.9 35.0 %collective-permute-start.25 = (bf16[256,1024]{1,0:T(8,128)(2,1)S(1)}, bf16[256,1024]{1,0:T(8,128)(2,1)S(1)}, u32[]{:S(2)}, u32[]{:S(2)}) collective-permute-start(bf16[256,1024]{1,0:T(8,128)(2,1)S(1)} %add_convert_fusion.4), channel_id=1, source_target_pairs={{0,4},{1,5},{2,6},{3,7},{4,0},{5,1},{6,2},{7,3},{8,12},{9,13},{10,... | collective-permute-start | bytes 1572872 | tf_op jit(solution)/shard_map/ppermute | solution.py:30
  216.2 26.8 %copy-start.14 = (bf16[256,256]{1,0:T(8,128)(2,1)}, bf16[256,256]{1,0:T(8,128)(2,1)S(1)}, u32[]{:S(2)}) copy-start(bf16[256,256]{1,0:T(8,128)(2,1)S(1)} %collective-permute-done.20.refs_1_) | copy-start | bytes 393220
  216.2 38.8 %collective-permute-start.24 = (bf16[512,256]{1,0:T(8,128)(2,1)S(1)}, bf16[512,256]{1,0:T(8,128)(2,1)S(1)}, u32[]{:S(2)}, u32[]{:S(2)}) collective-permute-start(bf16[512,256]{1,0:T(8,128)(2,1)S(1)} %constant_dynamic-update-slice_fusion), channel_id=1, source_target_pairs={{0,16},{8,24},{16,0},{24,8},{1,17},{9,25},{17,1},{25,9},{2,18},{10... | collective-permute-start | bytes 786440 | tf_op jit(solution)/shard_map/ppermute | solution.py:30
  235.9 16.4 %copy-start.9 = (bf16[768,1024]{1,0:T(8,128)(2,1)}, bf16[768,1024]{1,0:T(8,128)(2,1)S(1)}, u32[]{:S(2)}) copy-start(bf16[768,1024]{1,0:T(8,128)(2,1)S(1)} %collective-permute-done.26) | copy-start | bytes 4718596
  240.7 2.6 copy-start.8
  240.9 2.4 copy-start.18
  240.9 9.2 %collective-permute-start.28 = (bf16[256,1024]{1,0:T(8,128)(2,1)S(1)}, bf16[256,1024]{1,0:T(8,128)(2,1)S(1)}, u32[]{:S(2)}, u32[]{:S(2)}) collective-permute-start(bf16[256,1024]{1,0:T(8,128)(2,1)S(1)} %add_convert_fusion.3), channel_id=1, source_target_pairs={{0,8},{8,0},{16,24},{24,16},{1,9},{9,1},{17,25},{25,17},{2,10},{10... | collective-permute-start | bytes 1572872 | tf_op jit(solution)/shard_map/ppermute | solution.py:30
  243.0 4.9 %copy-start.1 = (f32[256,1024]{1,0:T(8,128)S(1)}, f32[256,1024]{1,0:T(8,128)}, u32[]{:S(2)}) copy-start(f32[256,1024]{1,0:T(8,128)} %fusion.48) | copy-start | bytes 3145732
  243.0 9.2 %collective-permute-start.29 = (bf16[256,1024]{1,0:T(8,128)(2,1)S(1)}, bf16[256,1024]{1,0:T(8,128)(2,1)S(1)}, u32[]{:S(2)}, u32[]{:S(2)}) collective-permute-start(bf16[256,1024]{1,0:T(8,128)(2,1)S(1)} %add_convert_fusion.2), channel_id=1, source_target_pairs={{0,16},{8,24},{16,0},{24,8},{1,17},{9,25},{17,1},{25,9},{2,18},{10... | collective-permute-start | bytes 1572872 | tf_op jit(solution)/shard_map/ppermute | solution.py:30
  245.4 30.8 %collective-permute-start.30 = (bf16[256,1024]{1,0:T(8,128)(2,1)}, bf16[256,1024]{1,0:T(8,128)(2,1)}, u32[]{:S(2)}, u32[]{:S(2)}) collective-permute-start(bf16[256,1024]{1,0:T(8,128)(2,1)} %add_convert_fusion.1), channel_id=1, source_target_pairs={{0,4},{1,5},{2,6},{3,7},{4,0},{5,1},{6,2},{7,3},{8,12},{9,13},{10,... | collective-permute-start | bytes 1572872 | tf_op jit(solution)/shard_map/ppermute | solution.py:30
  252.2 2.8 copy-start.23
  253.3 28.6 %collective-permute-start.31 = (bf16[256,1024]{1,0:T(8,128)(2,1)}, bf16[256,1024]{1,0:T(8,128)(2,1)}, u32[]{:S(2)}, u32[]{:S(2)}) collective-permute-start(bf16[256,1024]{1,0:T(8,128)(2,1)} %add_convert_fusion), channel_id=1, source_target_pairs={{0,4},{1,5},{2,6},{3,7},{4,0},{5,1},{6,2},{7,3},{8,12},{9,13},{10,... | collective-permute-start | bytes 1572872 | tf_op jit(solution)/shard_map/ppermute | solution.py:30
  271.7 10.2 %copy-start.2 = (f32[256,1024]{1,0:T(8,128)S(1)}, f32[256,1024]{1,0:T(8,128)}, u32[]{:S(2)}) copy-start(f32[256,1024]{1,0:T(8,128)} %fusion.50) | copy-start | bytes 3145732
  271.7 10.2 %copy-start.24 = (bf16[256,1024]{1,0:T(8,128)(2,1)S(1)}, bf16[256,1024]{1,0:T(8,128)(2,1)}, u32[]{:S(2)}) copy-start(bf16[256,1024]{1,0:T(8,128)(2,1)} %copy-done.23) | copy-start | bytes 1572868
  (7 other events, 6.6 us)
